TPU v7x, 32 devices: a whole 2x2x4 slice. The times are simulated.
32 devices in a mesh: fsdp: 16 (over z, y, core), tp: 2 (over x).
Axes of the slice: x: 2, y: 2, z: 4, core: 2. Of those that a mesh axis runs over, the one named last changes fastest.
Arguments:
- tokens: bfloat16 [9472, 768], P(('fsdp', 'tp')), may hold values from -6 to 6
- qkv_weight: bfloat16 [2, 768, 3, 768], P(None, 'fsdp', None, 'tp'), may hold values from -0.21875 to 0.21875
- out_weight: bfloat16 [2, 768, 768], P(None, 'tp', 'fsdp'), may hold values from -1.75 to 1.75
- up_weight: bfloat16 [2, 768, 3072], P(None, 'fsdp', 'tp'), may hold values from -0.21875 to 0.21875
- down_weight: bfloat16 [2, 3072, 768], P(None, 'tp', 'fsdp'), may hold values from -0.109375 to 0.109375
- norm_gain: float32 [2, 2, 768], replicated, may hold values from 0.5 to 1.5
- norm_shift: float32 [2, 2, 768], replicated, may hold values from -1.8 to 1.8
- qv_bias: float32 [2, 2, 768], replicated, may hold values from -1.8 to 1.8
- out_bias: float32 [2, 2, 768], replicated, may hold values from -1.8 to 1.8
- up_bias: float32 [2, 3072], replicated, may hold values from -1.8 to 1.8
- cotangent: bfloat16 [9472, 768], P(('fsdp', 'tp')), may hold values from -6 to 6
Outputs:
- activations: bfloat16 [9472, 768], P(('fsdp', 'tp'))
- input_grad: float32 [9472, 768], P(('fsdp', 'tp'))
- qkv_grad: float32 [2, 768, 3, 768], P(None, 'fsdp', None, 'tp')
- out_grad: float32 [2, 768, 768], P(None, 'tp', 'fsdp')
- up_grad: float32 [2, 768, 3072], P(None, 'fsdp', 'tp')
- down_grad: float32 [2, 3072, 768], P(None, 'tp', 'fsdp')
- gain_grad: float32 [2, 2, 768], replicated
- shift_grad: float32 [2, 2, 768], replicated
- qv_bias_grad: float32 [2, 2, 768], replicated
- out_bias_grad: float32 [2, 2, 768], replicated
- up_bias_grad: float32 [2, 3072], replicated
All inputs are finite; a program needn't handle non-finite values.
Results may differ from a plain program's by a relative error of at most 0.017.
Values may be sent and summed in bfloat16 or wider, within the bound.
No kernel may reach another device: no remote copies, remote signals or barrier semaphores. Data moves between devices by JAX's collectives and lax.ppermute only.
A program may use at most 128 MiB of HBM per device.

v0:
```python
from functools import partial

import jax
import jax.numpy as jnp
from jax import lax
from jax.sharding import PartitionSpec as P

D = 768
HEADS = 12
FF = 3072
SEQ = 197
LAYERS = 2
IMG_DEV = 3


def norm_rows(value, gain_vector, shift_vector):
    row_mean = jnp.mean(value, axis=-1, keepdims=True)
    centred = value - row_mean
    row_var = jnp.mean(centred * centred, axis=-1, keepdims=True)
    return centred * lax.rsqrt(row_var + 1e-06) * gain_vector + shift_vector


def row_product(left, right):
    return lax.dot_general(
        left, right, (((0,), (0,)), ((), ())), preferred_element_type=jnp.float32
    )


def back_product(left, right):
    return lax.dot_general(
        left, right, (((1,), (1,)), ((), ())), preferred_element_type=jnp.float32
    )


def fetch_weights(qkv_piece, out_piece, up_piece, down_piece):
    qkv_full, up_full = (
        lax.all_gather(qkv_piece, "fsdp", axis=0, tiled=True),
        lax.all_gather(up_piece, "fsdp", axis=0, tiled=True),
    )
    out_full, down_full = (
        lax.all_gather(out_piece, "fsdp", axis=1, tiled=True),
        lax.all_gather(down_piece, "fsdp", axis=1, tiled=True),
    )
    return (qkv_full, out_full, up_full, down_full)


def fetch_again(qkv_piece, out_piece, up_piece, down_piece):
    qkv_full, up_full = (
        lax.all_gather(qkv_piece, "fsdp", axis=0, tiled=True),
        lax.all_gather(up_piece, "fsdp", axis=0, tiled=True),
    )
    out_full, down_full = (
        lax.all_gather(out_piece, "fsdp", axis=1, tiled=True),
        lax.all_gather(down_piece, "fsdp", axis=1, tiled=True),
    )
    return (qkv_full, out_full, up_full, down_full)


def gather_rows(value):
    return lax.all_gather(value, "tp", axis=0, tiled=True)


def gather_grads(value):
    return lax.all_gather(value, "tp", axis=0, tiled=True)


def reduce_rows(left, weight, row_count):

    def partial_term(first_row, piece_rows):
        return jnp.dot(left, weight, preferred_element_type=jnp.float32)

    return lax.psum_scatter(
        partial_term(jnp.int32(0), lax.axis_size("tp") * row_count).astype(jnp.bfloat16),
        "tp",
        scatter_dimension=0,
        tiled=True,
    ).astype(jnp.float32)


def reduce_grads(left, weight, row_count):

    def partial_term(first_row, piece_rows):
        return back_product(left, weight)

    return lax.psum_scatter(
        partial_term(jnp.int32(0), lax.axis_size("tp") * row_count).astype(jnp.bfloat16),
        "tp",
        scatter_dimension=0,
        tiled=True,
    ).astype(jnp.float32)


def attend(queries, key_rows, values, images, local_heads, head_dim):
    grid_shape = (images, SEQ, local_heads, head_dim)
    scores = jnp.einsum(
        "ishd,ithd->ihst",
        queries.reshape(grid_shape),
        key_rows.reshape(grid_shape),
        preferred_element_type=jnp.float32,
    ) * head_dim ** (-0.5)
    row_max = jnp.max(scores, axis=-1, keepdims=True)
    expanded = jnp.exp(scores - row_max)
    row_total = jnp.sum(expanded, axis=-1, keepdims=True)
    soft_weights = (expanded / row_total).astype(jnp.bfloat16)
    log_total = row_max + jnp.log(row_total)
    mixed = jnp.einsum(
        "ihst,ithd->ishd",
        soft_weights,
        values.reshape(grid_shape),
        preferred_element_type=jnp.float32,
    )
    return (mixed.reshape(images * SEQ, local_heads * head_dim).astype(jnp.bfloat16), log_total)


def attend_back(mixed_grad, queries, key_rows, values, log_total, images, local_heads, head_dim):
    grid_shape = (images, SEQ, local_heads, head_dim)
    query_grid = queries.reshape(grid_shape)
    key_grid = key_rows.reshape(grid_shape)
    value_grid = values.reshape(grid_shape)
    grad_grid = mixed_grad.reshape(grid_shape)
    scale = head_dim ** (-0.5)
    scores = (
        jnp.einsum("ishd,ithd->ihst", query_grid, key_grid, preferred_element_type=jnp.float32)
        * scale
    )
    chances = jnp.exp(scores - log_total)
    soft_weights = chances.astype(jnp.bfloat16)
    value_grad = jnp.einsum(
        "ihst,ishd->ithd", soft_weights, grad_grid, preferred_element_type=jnp.float32
    ).astype(jnp.bfloat16)
    weight_grad = jnp.einsum(
        "ishd,ithd->ihst", grad_grid, value_grid, preferred_element_type=jnp.float32
    )
    score_grad = (
        chances * (weight_grad - jnp.sum(weight_grad * chances, axis=-1, keepdims=True))
    ).astype(jnp.bfloat16)
    query_grad = (
        jnp.einsum("ihst,ithd->ishd", score_grad, key_grid, preferred_element_type=jnp.float32)
        * scale
    ).astype(jnp.bfloat16)
    key_grad = (
        jnp.einsum("ihst,ishd->ithd", score_grad, query_grid, preferred_element_type=jnp.float32)
        * scale
    ).astype(jnp.bfloat16)
    flat_shape = (images * SEQ, local_heads * head_dim)
    return jnp.stack(
        [
            query_grad.reshape(flat_shape),
            key_grad.reshape(flat_shape),
            value_grad.reshape(flat_shape),
        ],
        axis=1,
    )


def on_device(
    tokens,
    qkv_weight,
    out_weight,
    up_weight,
    down_weight,
    norm_gain,
    norm_shift,
    qv_bias,
    out_bias,
    up_bias,
    cotangent,
):
    tp_index = lax.axis_index("tp")
    tp_count = lax.axis_size("tp")
    row_count = tokens.shape[0]
    local_width = qkv_weight.shape[3]
    inner_width = up_weight.shape[2]
    local_heads = HEADS // tp_count
    head_dim = D // HEADS
    images = IMG_DEV
    all_rows = images * SEQ
    slot_rows = row_count * tp_count
    live = (tp_index * row_count + jnp.arange(row_count) < all_rows)[:, None]

    def trimmed(value):
        return value[:all_rows]

    def padded(value):
        filler = jnp.zeros((slot_rows - all_rows,) + value.shape[1:], value.dtype)
        return jnp.concatenate([value, filler], axis=0)

    stream = tokens.astype(jnp.float32)
    saved_values = []
    for layer_index in range(LAYERS):
        qkv_full, out_full, up_full, down_full = fetch_weights(
            qkv_weight[layer_index],
            out_weight[layer_index],
            up_weight[layer_index],
            down_weight[layer_index],
        )
        local_qv = lax.dynamic_slice_in_dim(
            qv_bias[layer_index], tp_index * local_width, local_width, 1
        )
        local_up = lax.dynamic_slice_in_dim(
            up_bias[layer_index], tp_index * inner_width, inner_width, 0
        )
        layer_input = stream
        hidden = trimmed(
            gather_rows(
                norm_rows(stream, norm_gain[layer_index, 0], norm_shift[layer_index, 0]).astype(
                    jnp.bfloat16
                )
            )
        )
        projected = jnp.einsum("rd,dcn->rcn", hidden, qkv_full, preferred_element_type=jnp.float32)
        queries = (projected[:, 0] + local_qv[0]).astype(jnp.bfloat16)
        key_rows = projected[:, 1].astype(jnp.bfloat16)
        values = (projected[:, 2] + local_qv[1]).astype(jnp.bfloat16)
        mixed, log_total = attend(queries, key_rows, values, images, local_heads, head_dim)
        stream = stream + reduce_rows(padded(mixed), out_full, row_count) + out_bias[layer_index, 0]
        middle = stream
        hidden_two = trimmed(
            gather_rows(
                norm_rows(stream, norm_gain[layer_index, 1], norm_shift[layer_index, 1]).astype(
                    jnp.bfloat16
                )
            )
        )
        pre_gelu = jnp.dot(hidden_two, up_full, preferred_element_type=jnp.float32) + local_up
        activated = jax.nn.gelu(pre_gelu, approximate=False).astype(jnp.bfloat16)
        stream = (
            stream + reduce_rows(padded(activated), down_full, row_count) + out_bias[layer_index, 1]
        )
        saved_values.append(
            (
                layer_input,
                middle,
                hidden,
                queries,
                key_rows,
                values,
                mixed,
                log_total,
                hidden_two,
                pre_gelu,
                activated,
                (qkv_full, out_full, up_full, down_full),
            )
        )
    activations = jnp.where(live, stream, 0.0).astype(jnp.bfloat16)
    grad = jnp.where(live, cotangent.astype(jnp.float32), 0.0)
    matrix_grads = [None] * LAYERS
    gain_grads = [None] * LAYERS
    shift_grads = [None] * LAYERS
    qv_grads = [None] * LAYERS
    out_bias_grads = [None] * LAYERS
    up_bias_grads = [None] * LAYERS
    for layer_index in reversed(range(LAYERS)):
        (
            layer_input,
            middle,
            hidden,
            queries,
            key_rows,
            values,
            mixed,
            log_total,
            hidden_two,
            pre_gelu,
            activated,
            held,
        ) = saved_values[layer_index]
        qkv_full, out_full, up_full, down_full = fetch_again(
            qkv_weight[layer_index],
            out_weight[layer_index],
            up_weight[layer_index],
            down_weight[layer_index],
        )
        branch_grad = grad.astype(jnp.bfloat16)
        down_bias_grad = jnp.sum(branch_grad.astype(jnp.float32), axis=0)
        branch_full = trimmed(gather_grads(branch_grad))
        down_grad = row_product(activated, branch_full)
        act_grad = back_product(branch_full, down_full)
        gelu_value, gelu_back = jax.vjp(partial(jax.nn.gelu, approximate=False), pre_gelu)
        pre_grad = gelu_back(act_grad)[0].astype(jnp.bfloat16)
        up_vector_grad = jnp.sum(pre_grad.astype(jnp.float32), axis=0)
        up_grad = row_product(hidden_two, pre_grad)
        norm_grad = reduce_grads(padded(pre_grad), up_full, row_count)
        norm_value, norm_back = jax.vjp(
            norm_rows, middle, norm_gain[layer_index, 1], norm_shift[layer_index, 1]
        )
        middle_grad, gain_two, shift_two = norm_back(norm_grad)
        grad = grad + middle_grad
        branch_grad = grad.astype(jnp.bfloat16)
        attn_bias_grad = jnp.sum(branch_grad.astype(jnp.float32), axis=0)
        branch_full = trimmed(gather_grads(branch_grad))
        out_grad = row_product(mixed, branch_full)
        mixed_grad = back_product(branch_full, out_full).astype(jnp.bfloat16)
        stacked = attend_back(
            mixed_grad, queries, key_rows, values, log_total, images, local_heads, head_dim
        )
        stacked_sums = jnp.sum(stacked.astype(jnp.float32), axis=0)
        qkv_grad = jnp.einsum("rd,rcn->dcn", hidden, stacked, preferred_element_type=jnp.float32)
        norm_grad = reduce_grads(
            padded(stacked.reshape(all_rows, 3 * local_width)),
            qkv_full.reshape(D, 3 * local_width),
            row_count,
        )
        norm_value, norm_back = jax.vjp(
            norm_rows, layer_input, norm_gain[layer_index, 0], norm_shift[layer_index, 0]
        )
        input_part, gain_one, shift_one = norm_back(norm_grad)
        grad = grad + input_part
        qkv_owned, up_owned = (
            lax.psum_scatter(qkv_grad, "fsdp", scatter_dimension=0, tiled=True),
            lax.psum_scatter(up_grad, "fsdp", scatter_dimension=0, tiled=True),
        )
        out_owned, down_owned = (
            lax.psum_scatter(out_grad, "fsdp", scatter_dimension=1, tiled=True),
            lax.psum_scatter(down_grad, "fsdp", scatter_dimension=1, tiled=True),
        )
        matrix_grads[layer_index] = (qkv_owned, out_owned, up_owned, down_owned)
        gain_grads[layer_index] = jnp.stack([gain_one, gain_two])
        shift_grads[layer_index] = jnp.stack([shift_one, shift_two])
        qv_local = jnp.stack([stacked_sums[0], stacked_sums[2]])
        qv_grads[layer_index] = lax.dynamic_update_slice_in_dim(
            jnp.zeros((2, D), jnp.float32), qv_local, tp_index * local_width, 1
        )
        out_bias_grads[layer_index] = jnp.stack([attn_bias_grad, down_bias_grad])
        up_bias_grads[layer_index] = lax.dynamic_update_slice_in_dim(
            jnp.zeros((FF,), jnp.float32), up_vector_grad, tp_index * inner_width, 0
        )
    small_totals = lax.psum(
        (
            jnp.stack(gain_grads),
            jnp.stack(shift_grads),
            jnp.stack(qv_grads),
            jnp.stack(out_bias_grads),
            jnp.stack(up_bias_grads),
        ),
        ("fsdp", "tp"),
    )
    qkv_all = jnp.stack([entry[0] for entry in matrix_grads])
    out_all = jnp.stack([entry[1] for entry in matrix_grads])
    up_all = jnp.stack([entry[2] for entry in matrix_grads])
    down_all = jnp.stack([entry[3] for entry in matrix_grads])
    input_grad = jnp.where(live, grad, 0.0)
    return (
        activations,
        input_grad,
        qkv_all,
        out_all,
        up_all,
        down_all,
        small_totals[0],
        small_totals[1],
        small_totals[2],
        small_totals[3],
        small_totals[4],
    )


def solution(mesh):
    return jax.shard_map(
        on_device,
        mesh=mesh,
        in_specs=(
            P(("fsdp", "tp"), None),
            P(None, "fsdp", None, "tp"),
            P(None, "tp", "fsdp"),
            P(None, "fsdp", "tp"),
            P(None, "tp", "fsdp"),
            P(),
            P(),
            P(),
            P(),
            P(),
            P(("fsdp", "tp"), None),
        ),
        out_specs=(
            P(("fsdp", "tp"), None),
            P(("fsdp", "tp"), None),
            P(None, "fsdp", None, "tp"),
            P(None, "tp", "fsdp"),
            P(None, "fsdp", "tp"),
            P(None, "tp", "fsdp"),
            P(),
            P(),
            P(),
            P(),
            P(),
        ),
        check_vma=False,
    )
```

profile of v0, /device:TPU:0, one launch (start us, length us, event | category | flops | bytes accessed | tf_op | source)
XLA Modules:
  0.0 1309.1 jit_solution(1690009019639399178)
XLA Ops:
  17.3 14.1 %all_gather.56 = bf16[592,768]{1,0:T(8,128)(2,1)S(1)} all-gather(bf16[296,768]{1,0:T(8,128)(2,1)S(1)} %fusion.119), channel_id=1, replica_groups=mesh['fsdp'=16,'tp'=2] {'tp'}, dimensions={0}, use_global_device_ids=true | all-gather | bytes 1363968 | tf_op jit(solution)/shard_map/all_gather | solution.py:60
  31.4 26.4 %all-gather.1 = bf16[1,384,768]{1,2,0:T(8,128)(2,1)} all-gather(bf16[1,384,48]{1,2,0:T(8,128)(2,1)S(1)} %get-tuple-element.78), channel_id=3, replica_groups=mesh['fsdp'=16,'tp'=2] {'fsdp'}, dimensions={2}, use_global_device_ids=true | all-gather | bytes 626688 | tf_op jit(solution)/shard_map/all_gather | solution.py:41
  84.2 12.8 reduce-scatter.17.cloned.1.call-done
  101.0 24.6 %all_gather.59 = bf16[592,768]{1,0:T(8,128)(2,1)S(1)} all-gather(bf16[296,768]{1,0:T(8,128)(2,1)S(1)} %add_convert_fusion.8), channel_id=1, replica_groups=mesh['fsdp'=16,'tp'=2] {'tp'}, dimensions={0}, use_global_device_ids=true | all-gather | bytes 1363968 | tf_op jit(solution)/shard_map/all_gather | solution.py:60
  125.6 16.6 %all-gather.17.cloned.1.call-done = bf16[1,768,1536]{2,1,0:T(8,128)(2,1)} async-done(((bf16[1,48,1536]{2,1,0:T(8,128)(2,1)}), bf16[1,768,1536]{2,1,0:T(8,128)(2,1)}) %all-gather.17.cloned.1.call-update) | async-done | bytes 2359312 | tf_op jit(solution)/shard_map/all_gather | solution.py:38
  142.2 12.4 multiply_convert_fusion.3
  154.6 31.4 %all-gather.19.cloned.1.call-done = bf16[1,1536,768]{1,2,0:T(8,128)(2,1)} async-done(((bf16[1,1536,48]{1,2,0:T(8,128)(2,1)}), bf16[1,1536,768]{1,2,0:T(8,128)(2,1)}) %all-gather.19.cloned.1.call-update) | async-done | bytes 2359312 | tf_op jit(solution)/shard_map/all_gather | solution.py:42
  191.6 22.1 %all-gather.5 = bf16[1,384,768]{1,2,0:T(8,128)(2,1)} all-gather(bf16[1,384,48]{1,2,0:T(8,128)(2,1)S(1)} %get-tuple-element.77), channel_id=7, replica_groups=mesh['fsdp'=16,'tp'=2] {'fsdp'}, dimensions={2}, use_global_device_ids=true | all-gather | bytes 626688 | tf_op jit(solution)/shard_map/all_gather | solution.py:41
  216.1 13.3 %all_gather.62 = bf16[592,768]{1,0:T(8,128)(2,1)S(1)} all-gather(bf16[296,768]{1,0:T(8,128)(2,1)S(1)} %add_convert_fusion.7), channel_id=1, replica_groups=mesh['fsdp'=16,'tp'=2] {'tp'}, dimensions={0}, use_global_device_ids=true | all-gather | bytes 1363968 | tf_op jit(solution)/shard_map/all_gather | solution.py:60
  229.5 22.3 %all-gather.21.cloned.1.call-done = bf16[1,768,3,384]{3,1,2,0:T(8,128)(2,1)} async-done(((bf16[1,48,3,384]{3,1,2,0:T(8,128)(2,1)}), bf16[1,768,3,384]{3,1,2,0:T(8,128)(2,1)}) %all-gather.21.cloned.1.call-update) | async-done | bytes 1769488 | tf_op jit(solution)/shard_map/all_gather | solution.py:37
  285.6 22.4 %all_gather.68 = bf16[592,768]{1,0:T(8,128)(2,1)} all-gather(bf16[296,768]{1,0:T(8,128)(2,1)S(1)} %get-tuple-element.55), channel_id=1, replica_groups=mesh['fsdp'=16,'tp'=2] {'tp'}, dimensions={0}, use_global_device_ids=true | all-gather | bytes 1363968 | tf_op jit(solution)/shard_map/all_gather | solution.py:64
  310.5 12.6 all_gather.65
  323.2 30.4 %all-gather.23.cloned.1.call-done = bf16[1,768,1536]{2,1,0:T(8,128)(2,1)} async-done(((bf16[1,48,1536]{2,1,0:T(8,128)(2,1)}), bf16[1,768,1536]{2,1,0:T(8,128)(2,1)}) %all-gather.23.cloned.1.call-update) | async-done | bytes 2359312 | tf_op jit(solution)/shard_map/all_gather | solution.py:38
  353.6 12.6 multiply_convert_fusion.2
  366.2 30.7 %all-gather.25.cloned.1.call-done = bf16[1,1536,768]{1,2,0:T(8,128)(2,1)} async-done(((bf16[1,1536,48]{1,2,0:T(8,128)(2,1)}), bf16[1,1536,768]{1,2,0:T(8,128)(2,1)}) %all-gather.25.cloned.1.call-update) | async-done | bytes 2359312 | tf_op jit(solution)/shard_map/all_gather | solution.py:42
  396.9 7.3 convert_reduce_fusion
  417.6 8.2 reduce-scatter.25.cloned.1.call-done
  429.1 17.9 %reduce-scatter.23.cloned.1.call-done = bf16[296,768]{1,0:T(8,128)(2,1)} async-done(((bf16[592,768]{1,0:T(8,128)(2,1)}), bf16[296,768]{1,0:T(8,128)(2,1)}) %reduce-scatter.23.cloned.1.call-update) | async-done | bytes 454672 | tf_op jit(solution)/shard_map/reduce_scatter | solution.py:72
  452.3 12.8 all_gather.69
  500.5 19.0 %reduce-scatter.27.cloned.1.call-done = bf16[296,768]{1,0:T(8,128)(2,1)} async-done(((bf16[592,768]{1,0:T(8,128)(2,1)}), bf16[296,768]{1,0:T(8,128)(2,1)}) %reduce-scatter.27.cloned.1.call-update) | async-done | bytes 454672 | tf_op jit(solution)/shard_map/reduce_scatter | solution.py:85
  526.3 12.9 all_gather.70
  555.2 11.9 reduce-scatter.29.cloned.1.call-done
  573.6 12.8 all_gather.71
  670.5 19.0 %reduce-scatter.37.cloned.1.call-done = f32[384,48]{0,1:T(8,128)} async-done(((f32[384,768]{0,1:T(8,128)}), f32[384,48]{0,1:T(8,128)}) %reduce-scatter.37.cloned.1.call-update) | async-done | bytes 73744 | tf_op jit(solution)/shard_map/reduce_scatter | solution.py:315
  691.1 19.0 %reduce-scatter.31.cloned.1.call-done = bf16[296,768]{1,0:T(8,128)(2,1)} async-done(((bf16[592,768]{1,0:T(8,128)(2,1)}), bf16[296,768]{1,0:T(8,128)(2,1)}) %reduce-scatter.31.cloned.1.call-update) | async-done | bytes 454672 | tf_op jit(solution)/shard_map/reduce_scatter | solution.py:85
  717.2 72.2 %reduce-scatter.47.cloned.1.call-done = f32[1536,48]{0,1:T(8,128)} async-done(((f32[1536,768]{0,1:T(8,128)}), f32[1536,48]{0,1:T(8,128)}) %reduce-scatter.47.cloned.1.call-update) | async-done | bytes 294928 | tf_op jit(solution)/shard_map/reduce_scatter | solution.py:316
  789.4 78.5 %reduce-scatter.45.cloned.1.call-done = f32[1536,48]{0,1:T(8,128)} async-done(((f32[1536,768]{0,1:T(8,128)}), f32[1536,48]{0,1:T(8,128)}) %reduce-scatter.45.cloned.1.call-update) | async-done | bytes 294928 | tf_op jit(solution)/shard_map/reduce_scatter | solution.py:316
  869.8 76.7 %reduce-scatter.43.cloned.1.call-done = f32[48,1536]{1,0:T(8,128)} async-done(((f32[768,1536]{1,0:T(8,128)}), f32[48,1536]{1,0:T(8,128)}) %reduce-scatter.43.cloned.1.call-update) | async-done | bytes 294928 | tf_op jit(solution)/shard_map/reduce_scatter | solution.py:312
  946.5 78.5 %reduce-scatter.41.cloned.1.call-done = f32[48,1536]{1,0:T(8,128)} async-done(((f32[768,1536]{1,0:T(8,128)}), f32[48,1536]{1,0:T(8,128)}) %reduce-scatter.41.cloned.1.call-update) | async-done | bytes 294928 | tf_op jit(solution)/shard_map/reduce_scatter | solution.py:312
  1026.9 69.3 %reduce-scatter.35.cloned.1.call-done = f32[48,3,384]{2,0,1:T(8,128)} async-done(((f32[768,3,384]{2,0,1:T(8,128)}), f32[48,3,384]{2,0,1:T(8,128)}) %reduce-scatter.35.cloned.1.call-update) | async-done | bytes 221200 | tf_op jit(solution)/shard_map/reduce_scatter | solution.py:311
  1096.3 70.8 %reduce-scatter.33.cloned.1.call-done = f32[48,3,384]{2,0,1:T(8,128)} async-done(((f32[768,3,384]{2,0,1:T(8,128)}), f32[48,3,384]{2,0,1:T(8,128)}) %reduce-scatter.33.cloned.1.call-update) | async-done | bytes 221200 | tf_op jit(solution)/shard_map/reduce_scatter | solution.py:311
  1168.9 126.9 %all-reduce.11.cloned.1.call-done = (f32[2,2,768]{2,1,0:T(2,128)}, f32[2,2,768]{2,1,0:T(2,128)}, f32[2,2,768]{2,1,0:T(2,128)}, f32[2,2,768]{2,1,0:T(2,128)}, f32[2,3072]{1,0:T(2,128)}) async-done(((f32[2,2,768]{2,1,0:T(2,128)}, f32[2,2,768]{2,1,0:T(2,128)}, f32[2,2,768]{2,1,0:T(2,128)}, f32[2,2,768]{2,1,0:T(2,128)}, f32[2,3072]{1,0:T(2,128)}), (f32[2,2,768]{2,1,0:T(2,128)}, f32[2,2,768]{2,1,0:T(2,128)}, ...) | async-done | bytes 73744 | tf_op jit(solution)/shard_map/psum | solution.py:329
  (453 shorter events, 274.9 us)
Async XLA Ops:
  7.2 50.5 %all-gather.15.cloned.1.call-start = ((), (), s32[]{:S(2)}) async-start(), calls=%async_computation.32 | async-start | bytes 1880064 | tf_op jit(solution)/shard_map/all_gather | solution.py:37
  8.9 88.1 %reduce-scatter.17.cloned.1.call-start = ((), (), s32[]{:S(2)}) async-start(), calls=%async_computation.16 | async-start | bytes 1363968 | tf_op jit(solution)/shard_map/reduce_scatter | solution.py:72
  11.3 49.2 %copy-start.48 = (f32[768]{0:T(1024)}, f32[768]{0:T(1024)S(1)}, u32[]{:S(2)}) copy-start(f32[768]{0:T(1024)S(1)} %get-tuple-element.32) | copy-start | bytes 9220
  81.2 61.0 %all-gather.17.cloned.1.call-start = ((), (), s32[]{:S(2)}) async-start(), calls=%async_computation.33 | async-start | bytes 2506752 | tf_op jit(solution)/shard_map/all_gather | solution.py:38
  82.0 104.0 %all-gather.19.cloned.1.call-start = ((), (), s32[]{:S(2)}) async-start(), calls=%async_computation.34 | async-start | bytes 2506752 | tf_op jit(solution)/shard_map/all_gather | solution.py:42
  82.8 130.9 %reduce-scatter.19.cloned.1.call-start = ((), (), s32[]{:S(2)}) async-start(), calls=%async_computation.17 | async-start | bytes 1363968 | tf_op jit(solution)/shard_map/reduce_scatter | solution.py:72
  99.6 55.0 %copy-start.75 = (f32[296]{0:T(512)}, f32[296]{0:T(512)S(1)}, u32[]{:S(2)}) copy-start(f32[296]{0:T(512)S(1)} %multiply_reduce_fusion.6) | copy-start | bytes 3556
  99.6 55.0 %copy-start.58 = (f32[296]{0:T(512)}, f32[296]{0:T(512)S(1)}, u32[]{:S(2)}) copy-start(f32[296]{0:T(512)S(1)} %fusion.177) | copy-start | bytes 3556
  190.8 60.9 %all-gather.21.cloned.1.call-start = ((), (), s32[]{:S(2)}) async-start(), calls=%async_computation.35 | async-start | bytes 1880064 | tf_op jit(solution)/shard_map/all_gather | solution.py:37
  191.4 117.3 %reduce-scatter.21.cloned.1.call-start = ((), (), s32[]{:S(2)}) async-start(), calls=%async_computation.18 | async-start | bytes 1363968 | tf_op jit(solution)/shard_map/reduce_scatter | solution.py:72
  281.7 71.9 %all-gather.23.cloned.1.call-start = ((), (), s32[]{:S(2)}) async-start(), calls=%async_computation.36 | async-start | bytes 2506752 | tf_op jit(solution)/shard_map/all_gather | solution.py:38
  282.4 114.5 %all-gather.25.cloned.1.call-start = ((), (), s32[]{:S(2)}) async-start(), calls=%async_computation.37 | async-start | bytes 2506752 | tf_op jit(solution)/shard_map/all_gather | solution.py:42
  283.2 142.6 %reduce-scatter.25.cloned.1.call-start = ((), (), s32[]{:S(2)}) async-start(), calls=%async_computation.20 | async-start | bytes 1363968 | tf_op jit(solution)/shard_map/reduce_scatter | solution.py:85
  310.0 56.2 %copy-start.61 = (f32[296]{0:T(512)}, f32[296]{0:T(512)S(1)}, u32[]{:S(2)}) copy-start(f32[296]{0:T(512)S(1)} %broadcast_multiply_fusion) | copy-start | bytes 3556
  310.2 55.9 %copy-start.79 = (f32[296]{0:T(512)}, f32[296]{0:T(512)S(1)}, u32[]{:S(2)}) copy-start(f32[296]{0:T(512)S(1)} %multiply_reduce_fusion.4) | copy-start | bytes 3556
  310.3 55.9 %copy-start.68 = (f32[296]{0:T(512)}, f32[296]{0:T(512)S(1)}, u32[]{:S(2)}) copy-start(f32[296]{0:T(512)S(1)} %fusion.179) | copy-start | bytes 3556
  408.1 38.9 %reduce-scatter.23.cloned.1.call-start = ((), (), s32[]{:S(2)}) async-start(), calls=%async_computation.19 | async-start | bytes 1363968 | tf_op jit(solution)/shard_map/reduce_scatter | solution.py:72
  412.9 106.5 %reduce-scatter.27.cloned.1.call-start = ((), (), s32[]{:S(2)}) async-start(), calls=%async_computation.21 | async-start | bytes 1363968 | tf_op jit(solution)/shard_map/reduce_scatter | solution.py:85
  500.4 66.7 %reduce-scatter.29.cloned.1.call-start = ((), (), s32[]{:S(2)}) async-start(), calls=%async_computation.22 | async-start | bytes 1363968 | tf_op jit(solution)/shard_map/reduce_scatter | solution.py:85
  548.1 122.3 %reduce-scatter.39.cloned.1.call-start = ((), (), s32[]{:S(2)}) async-start(), calls=%async_computation.27 | async-start | bytes 1253376 | tf_op jit(solution)/shard_map/reduce_scatter | solution.py:315
  555.2 134.4 %reduce-scatter.37.cloned.1.call-start = ((), (), s32[]{:S(2)}) async-start(), calls=%async_computation.26 | async-start | bytes 1253376 | tf_op jit(solution)/shard_map/reduce_scatter | solution.py:315
  595.8 114.3 %reduce-scatter.31.cloned.1.call-start = ((), (), s32[]{:S(2)}) async-start(), calls=%async_computation.23 | async-start | bytes 1363968 | tf_op jit(solution)/shard_map/reduce_scatter | solution.py:85
  628.6 160.8 %reduce-scatter.47.cloned.1.call-start = ((), (), s32[]{:S(2)}) async-start(), calls=%async_computation.31 | async-start | bytes 5013504 | tf_op jit(solution)/shard_map/reduce_scatter | solution.py:316
  634.3 233.5 %reduce-scatter.45.cloned.1.call-start = ((), (), s32[]{:S(2)}) async-start(), calls=%async_computation.30 | async-start | bytes 5013504 | tf_op jit(solution)/shard_map/reduce_scatter | solution.py:316
  641.3 305.3 %reduce-scatter.43.cloned.1.call-start = ((), (), s32[]{:S(2)}) async-start(), calls=%async_computation.29 | async-start | bytes 5013504 | tf_op jit(solution)/shard_map/reduce_scatter | solution.py:312
  648.3 376.8 %reduce-scatter.41.cloned.1.call-start = ((), (), s32[]{:S(2)}) async-start(), calls=%async_computation.28 | async-start | bytes 5013504 | tf_op jit(solution)/shard_map/reduce_scatter | solution.py:312
  655.1 441.1 %reduce-scatter.35.cloned.1.call-start = ((), (), s32[]{:S(2)}) async-start(), calls=%async_computation.25 | async-start | bytes 3760128 | tf_op jit(solution)/shard_map/reduce_scatter | solution.py:311
  661.2 505.9 %reduce-scatter.33.cloned.1.call-start = ((), (), s32[]{:S(2)}) async-start(), calls=%async_computation.24 | async-start | bytes 3760128 | tf_op jit(solution)/shard_map/reduce_scatter | solution.py:311
  666.2 48.2 %copy-start.7 = (f32[296,768]{1,0:T(8,128)S(1)}, f32[296,768]{1,0:T(8,128)}, u32[]{:S(2)}) copy-start(f32[296,768]{1,0:T(8,128)} %copy-done.6) | copy-start | bytes 2727940
  666.2 48.2 %copy-start.60 = (f32[296]{0:T(512)S(1)}, f32[296]{0:T(512)}, u32[]{:S(2)}) copy-start(f32[296]{0:T(512)} %copy-done.58) | copy-start | bytes 3556
  666.3 48.2 %copy-start.67 = (f32[296]{0:T(512)S(1)}, f32[296]{0:T(512)}, u32[]{:S(2)}) copy-start(f32[296]{0:T(512)} %copy-done.66) | copy-start | bytes 3556
  666.3 629.5 %all-reduce.11.cloned.1.call-start = ((), (), s32[]{:S(2)}) async-start(), calls=%async_computation.38 | async-start | bytes 147456 | tf_op jit(solution)/shard_map/psum | solution.py:329
  (97 other events, 1296.6 us)
Sparse Core Ops, SparseCore 0:
  10.9 44.6 all-gather.14
  81.3 15.6 reduce-scatter.16
  99.9 42.2 all-gather.16
  144.9 41.0 all-gather.18
  190.9 17.5 reduce-scatter.18
  211.3 40.4 all-gather.20
  281.8 26.8 reduce-scatter.20
  311.6 41.9 all-gather.22
  355.9 41.0 all-gather.24
  408.2 17.5 reduce-scatter.24
  428.0 18.8 reduce-scatter.22
  500.6 18.8 reduce-scatter.26
  548.2 18.8 reduce-scatter.28
  570.6 58.1 reduce-scatter.38
  632.3 57.1 reduce-scatter.36
  692.2 17.8 reduce-scatter.30
  713.8 75.5 reduce-scatter.46
  793.1 74.7 reduce-scatter.44
  871.7 74.7 reduce-scatter.42
  950.2 74.7 reduce-scatter.40
  1028.9 67.3 reduce-scatter.34
  1100.1 66.9 reduce-scatter.32
  1174.7 121.1 all-reduce.10
where the time goes:
time: 1320 us; the launch traced here: 1310 us
  waiting for transfers between devices  815 us (62%)
  blocking collectives  174 us (13%)
  matrix products  133 us (10%)
  local copies, waits for them, and re-layouts  105 us (8%)
  other arithmetic  64.3 us (5%)
  between operations  15.7 us (1%)
    reduce_scatter x2, waiting for transfers between devices, on_device(): lax.psum_scatter(up_grad, 'fsdp', scatter_dimension=0, tiled=True)  155 us
    reduce_scatter x2, waiting for transfers between devices, on_device(): lax.psum_scatter(down_grad, 'fsdp', scatter_dimension=1, tiled=True)  151 us
    reduce_scatter x2, waiting for transfers between devices, on_device(): lax.psum_scatter(qkv_grad, 'fsdp', scatter_dimension=0, tiled=True)  140 us
    psum x1, waiting for transfers between devices, on_device(): lax.psum((jnp.stack(gain_grads), jnp.stack(shift_grads), jnp.stack(qv_gra...  127 us
    all_gather x4, blocking collectives, gather_rows(): return lax.all_gather(value, 'tp', axis=0, tiled=True)  64.7 us
    all_gather x2, waiting for transfers between devices, fetch_weights(): lax.all_gather(down_piece, 'fsdp', axis=1, tiled=True)  62.1 us
    all_gather x4, blocking collectives, gather_grads(): return lax.all_gather(value, 'tp', axis=0, tiled=True)  60.9 us
    reduce_scatter x4, waiting for transfers between devices, reduce_grads(): lax.psum_scatter(partial_term(jnp.int32(0), lax.axis_size('tp') * row_cou...  58.1 us
  transfers between devices with their start and end apart: 23, of which 20 were waited for; matrix products, arithmetic and copies ran while one was open for 12% of the time, Pallas kernels for 0%

commit v1 on v0

v1 whole, which is shorter than its diff:
```python
from functools import partial

import jax
import jax.numpy as jnp
from jax import lax
from jax.sharding import PartitionSpec as P

D = 768
HEADS = 12
FF = 3072
SEQ = 197
LAYERS = 2
IMG_DEV = 3


def norm_rows(value, gain_vector, shift_vector):
    row_mean = jnp.mean(value, axis=-1, keepdims=True)
    centred = value - row_mean
    row_var = jnp.mean(centred * centred, axis=-1, keepdims=True)
    return centred * lax.rsqrt(row_var + 1e-06) * gain_vector + shift_vector


def row_product(left, right):
    return lax.dot_general(
        left, right, (((0,), (0,)), ((), ())), preferred_element_type=jnp.float32
    )


def back_product(left, right):
    return lax.dot_general(
        left, right, (((1,), (1,)), ((), ())), preferred_element_type=jnp.float32
    )


def halves(own, other, first):
    return jnp.concatenate(
        [jnp.where(first, own, other), jnp.where(first, other, own)], axis=0
    )


def swap(value):
    return lax.ppermute(value, "tp", [(0, 1), (1, 0)])


def summed_everywhere(value, fsdp_count):
    step = 1
    while step < fsdp_count:
        value = value + lax.ppermute(
            value, "fsdp", [(place, place ^ step) for place in range(fsdp_count)]
        )
        step *= 2
    return value + swap(value)


def gathered(pieces):
    return lax.all_gather(jnp.concatenate(pieces, axis=1), "fsdp", axis=0, tiled=True)


def scattered(pieces):
    joined = jnp.concatenate([piece.astype(jnp.bfloat16) for piece in pieces], axis=1)
    return lax.psum_scatter(joined, "fsdp", scatter_dimension=0, tiled=True).astype(jnp.float32)


def attend(queries, key_rows, values, images, local_heads, head_dim):
    grid_shape = (images, SEQ, local_heads, head_dim)
    scores = jnp.einsum(
        "ishd,ithd->ihst",
        queries.reshape(grid_shape),
        key_rows.reshape(grid_shape),
        preferred_element_type=jnp.float32,
    ) * head_dim ** (-0.5)
    row_max = jnp.max(scores, axis=-1, keepdims=True)
    expanded = jnp.exp(scores - row_max)
    row_total = jnp.sum(expanded, axis=-1, keepdims=True)
    soft_weights = (expanded / row_total).astype(jnp.bfloat16)
    log_total = row_max + jnp.log(row_total)
    mixed = jnp.einsum(
        "ihst,ithd->ishd",
        soft_weights,
        values.reshape(grid_shape),
        preferred_element_type=jnp.float32,
    )
    return (mixed.reshape(images * SEQ, local_heads * head_dim).astype(jnp.bfloat16), log_total)


def attend_back(mixed_grad, queries, key_rows, values, log_total, images, local_heads, head_dim):
    grid_shape = (images, SEQ, local_heads, head_dim)
    query_grid = queries.reshape(grid_shape)
    key_grid = key_rows.reshape(grid_shape)
    value_grid = values.reshape(grid_shape)
    grad_grid = mixed_grad.reshape(grid_shape)
    scale = head_dim ** (-0.5)
    scores = (
        jnp.einsum("ishd,ithd->ihst", query_grid, key_grid, preferred_element_type=jnp.float32)
        * scale
    )
    chances = jnp.exp(scores - log_total)
    soft_weights = chances.astype(jnp.bfloat16)
    value_grad = jnp.einsum(
        "ihst,ishd->ithd", soft_weights, grad_grid, preferred_element_type=jnp.float32
    ).astype(jnp.bfloat16)
    weight_grad = jnp.einsum(
        "ishd,ithd->ihst", grad_grid, value_grid, preferred_element_type=jnp.float32
    )
    score_grad = (
        chances * (weight_grad - jnp.sum(weight_grad * chances, axis=-1, keepdims=True))
    ).astype(jnp.bfloat16)
    query_grad = (
        jnp.einsum("ihst,ithd->ishd", score_grad, key_grid, preferred_element_type=jnp.float32)
        * scale
    ).astype(jnp.bfloat16)
    key_grad = (
        jnp.einsum("ihst,ishd->ithd", score_grad, query_grid, preferred_element_type=jnp.float32)
        * scale
    ).astype(jnp.bfloat16)
    flat_shape = (images * SEQ, local_heads * head_dim)
    return jnp.stack(
        [
            query_grad.reshape(flat_shape),
            key_grad.reshape(flat_shape),
            value_grad.reshape(flat_shape),
        ],
        axis=1,
    )


def on_device(
    tokens,
    qkv_weight,
    out_weight,
    up_weight,
    down_weight,
    norm_gain,
    norm_shift,
    qv_bias,
    out_bias,
    up_bias,
    cotangent,
):
    tp_index = lax.axis_index("tp")
    tp_count = lax.axis_size("tp")
    fsdp_count = lax.axis_size("fsdp")
    row_count = tokens.shape[0]
    local_width = qkv_weight.shape[3]
    inner_width = up_weight.shape[2]
    piece_rows = qkv_weight.shape[1]
    local_heads = HEADS // tp_count
    head_dim = D // HEADS
    images = IMG_DEV
    all_rows = images * SEQ
    slot_rows = row_count * tp_count
    first = tp_index == 0
    live = (tp_index * row_count + jnp.arange(row_count) < all_rows)[:, None]
    cut_qkv = 3 * local_width
    cut_out = cut_qkv + local_width
    cut_up = cut_out + inner_width
    cut_down = cut_up + inner_width

    def padded(value):
        filler = jnp.zeros((slot_rows - all_rows,) + value.shape[1:], value.dtype)
        return jnp.concatenate([value, filler], axis=0)

    def own_rows(value):
        return lax.dynamic_slice_in_dim(value, tp_index * row_count, row_count, 0)

    def other_rows(value):
        return lax.dynamic_slice_in_dim(value, (1 - tp_index) * row_count, row_count, 0)

    def shared_sum(product, own_left, other_left, weight):
        sent = swap(product(other_left, weight).astype(jnp.bfloat16))
        return product(own_left, weight) + sent.astype(jnp.float32)

    def plain(left, right):
        return jnp.dot(left, right, preferred_element_type=jnp.float32)

    def attn_pieces(layer_index):
        return [
            qkv_weight[layer_index].reshape(piece_rows, cut_qkv),
            out_weight[layer_index].T,
        ]

    def mlp_pieces(layer_index):
        return [up_weight[layer_index], down_weight[layer_index].T]

    attn_zero = gathered(attn_pieces(0))
    mlp_zero = gathered(mlp_pieces(0))
    full_one = gathered(attn_pieces(1) + mlp_pieces(1))
    weights = [
        (
            attn_zero[:, :cut_qkv],
            attn_zero[:, cut_qkv:],
            mlp_zero[:, :inner_width],
            mlp_zero[:, inner_width:],
        ),
        (
            full_one[:, :cut_qkv],
            full_one[:, cut_qkv:cut_out],
            full_one[:, cut_out:cut_up],
            full_one[:, cut_up:cut_down],
        ),
    ]

    stream = tokens.astype(jnp.float32)
    saved_values = []
    for layer_index in range(LAYERS):
        qkv_full, out_turned, up_full, down_turned = weights[layer_index]
        local_qv = lax.dynamic_slice_in_dim(
            qv_bias[layer_index], tp_index * local_width, local_width, 1
        )
        local_up = lax.dynamic_slice_in_dim(
            up_bias[layer_index], tp_index * inner_width, inner_width, 0
        )
        layer_input = stream
        own_hidden = norm_rows(
            stream, norm_gain[layer_index, 0], norm_shift[layer_index, 0]
        ).astype(jnp.bfloat16)
        hidden = halves(own_hidden, swap(own_hidden), first)
        projected = plain(hidden, qkv_full)[:all_rows]
        queries = (projected[:, :local_width] + local_qv[0]).astype(jnp.bfloat16)
        key_rows = projected[:, local_width : 2 * local_width].astype(jnp.bfloat16)
        values = (projected[:, 2 * local_width :] + local_qv[1]).astype(jnp.bfloat16)
        mixed, log_total = attend(queries, key_rows, values, images, local_heads, head_dim)
        mixed = padded(mixed)
        stream = (
            stream
            + shared_sum(back_product, own_rows(mixed), other_rows(mixed), out_turned)
            + out_bias[layer_index, 0]
        )
        middle = stream
        hidden_own = norm_rows(
            stream, norm_gain[layer_index, 1], norm_shift[layer_index, 1]
        ).astype(jnp.bfloat16)
        hidden_other = swap(hidden_own)
        pre_own = plain(hidden_own, up_full) + local_up
        pre_other = plain(hidden_other, up_full) + local_up
        act_other = jax.nn.gelu(pre_other, approximate=False).astype(jnp.bfloat16)
        act_own = jax.nn.gelu(pre_own, approximate=False).astype(jnp.bfloat16)
        stream = (
            stream
            + shared_sum(back_product, act_own, act_other, down_turned)
            + out_bias[layer_index, 1]
        )
        saved_values.append(
            (
                layer_input,
                middle,
                hidden,
                queries,
                key_rows,
                values,
                mixed,
                log_total,
                jnp.concatenate([hidden_own, hidden_other], axis=0),
                pre_own,
                pre_other,
                jnp.concatenate([act_own, act_other], axis=0),
            )
        )
    activations = jnp.where(live, stream, 0.0).astype(jnp.bfloat16)
    grad = jnp.where(live, cotangent.astype(jnp.float32), 0.0)
    owned = []
    gain_grads = [None] * LAYERS
    shift_grads = [None] * LAYERS
    qv_grads = [None] * LAYERS
    out_bias_grads = [None] * LAYERS
    up_bias_grads = [None] * LAYERS
    for layer_index in reversed(range(LAYERS)):
        (
            layer_input,
            middle,
            hidden,
            queries,
            key_rows,
            values,
            mixed,
            log_total,
            hidden_two,
            pre_own,
            pre_other,
            activated,
        ) = saved_values[layer_index]
        qkv_full, out_turned, up_full, down_turned = weights[layer_index]
        branch_own = grad.astype(jnp.bfloat16)
        down_bias_grad = jnp.sum(branch_own.astype(jnp.float32), axis=0)
        branch_other = swap(branch_own)

        def through_gelu(branch, pre):
            act_grad = plain(branch, down_turned)
            gelu_back = jax.vjp(partial(jax.nn.gelu, approximate=False), pre)[1]
            return gelu_back(act_grad)[0].astype(jnp.bfloat16)

        du_own = through_gelu(branch_own, pre_own)
        du_other = through_gelu(branch_other, pre_other)
        norm_grad = shared_sum(back_product, du_own, du_other, up_full)
        pre_grad = jnp.concatenate([du_own, du_other], axis=0)
        branch_both = jnp.concatenate([branch_own, branch_other], axis=0)
        down_grad = row_product(branch_both, activated)
        up_vector_grad = jnp.sum(pre_grad.astype(jnp.float32), axis=0)
        up_grad = row_product(hidden_two, pre_grad)
        norm_back = jax.vjp(
            norm_rows, middle, norm_gain[layer_index, 1], norm_shift[layer_index, 1]
        )[1]
        middle_grad, gain_two, shift_two = norm_back(norm_grad)
        grad = grad + middle_grad
        branch_own = grad.astype(jnp.bfloat16)
        attn_bias_grad = jnp.sum(branch_own.astype(jnp.float32), axis=0)
        branch_full = halves(branch_own, swap(branch_own), first)
        out_grad = row_product(branch_full, mixed)
        mixed_grad = plain(branch_full, out_turned).astype(jnp.bfloat16)[:all_rows]
        stacked = attend_back(
            mixed_grad, queries, key_rows, values, log_total, images, local_heads, head_dim
        )
        stacked = padded(stacked.reshape(all_rows, 3 * local_width))
        stacked_sums = jnp.sum(stacked.astype(jnp.float32), axis=0).reshape(3, local_width)
        norm_grad = shared_sum(back_product, own_rows(stacked), other_rows(stacked), qkv_full)
        qkv_grad = row_product(hidden, stacked)
        norm_back = jax.vjp(
            norm_rows, layer_input, norm_gain[layer_index, 0], norm_shift[layer_index, 0]
        )[1]
        input_part, gain_one, shift_one = norm_back(norm_grad)
        grad = grad + input_part
        if layer_index:
            owned.append(
                (scattered([up_grad, down_grad]), scattered([qkv_grad, out_grad]))
            )
        else:
            joined = scattered([up_grad, down_grad, qkv_grad, out_grad])
            owned.append((joined[:, : 2 * inner_width], joined[:, 2 * inner_width :]))
        gain_grads[layer_index] = jnp.stack([gain_one, gain_two])
        shift_grads[layer_index] = jnp.stack([shift_one, shift_two])
        qv_local = jnp.stack([stacked_sums[0], stacked_sums[2]])
        qv_grads[layer_index] = lax.dynamic_update_slice_in_dim(
            jnp.zeros((2, D), jnp.float32), qv_local, tp_index * local_width, 1
        )
        out_bias_grads[layer_index] = jnp.stack([attn_bias_grad, down_bias_grad])
        up_bias_grads[layer_index] = lax.dynamic_update_slice_in_dim(
            jnp.zeros((FF,), jnp.float32), up_vector_grad, tp_index * inner_width, 0
        ).reshape(FF // D, D)
    small = jnp.concatenate(
        gain_grads + shift_grads + qv_grads + out_bias_grads + up_bias_grads, axis=0
    )
    small = summed_everywhere(small, fsdp_count)
    pair = 2 * LAYERS
    small_totals = [small[pair * k : pair * (k + 1)].reshape(LAYERS, 2, D) for k in range(4)]
    up_totals = small[4 * pair :].reshape(LAYERS, FF)
    owned = owned[::-1]
    up_all = jnp.stack([mlp[:, :inner_width] for mlp, attn in owned])
    down_all = jnp.stack([mlp[:, inner_width:].T for mlp, attn in owned])
    qkv_all = jnp.stack(
        [attn[:, :cut_qkv].reshape(piece_rows, 3, local_width) for mlp, attn in owned]
    )
    out_all = jnp.stack([attn[:, cut_qkv:].T for mlp, attn in owned])
    input_grad = jnp.where(live, grad, 0.0)
    return (
        activations,
        input_grad,
        qkv_all,
        out_all,
        up_all,
        down_all,
        small_totals[0],
        small_totals[1],
        small_totals[2],
        small_totals[3],
        up_totals,
    )


def solution(mesh):
    return jax.shard_map(
        on_device,
        mesh=mesh,
        in_specs=(
            P(("fsdp", "tp"), None),
            P(None, "fsdp", None, "tp"),
            P(None, "tp", "fsdp"),
            P(None, "fsdp", "tp"),
            P(None, "tp", "fsdp"),
            P(),
            P(),
            P(),
            P(),
            P(),
            P(("fsdp", "tp"), None),
        ),
        out_specs=(
            P(("fsdp", "tp"), None),
            P(("fsdp", "tp"), None),
            P(None, "fsdp", None, "tp"),
            P(None, "tp", "fsdp"),
            P(None, "fsdp", "tp"),
            P(None, "tp", "fsdp"),
            P(),
            P(),
            P(),
            P(),
            P(),
        ),
        check_vma=False,
    )
```

time: 1320 us -> 555 us (0.42)
  waiting for transfers between devices: 815 us -> 296 us
  blocking collectives: 174 us -> 0 us
  local copies, waits for them, and re-layouts: 105 us -> 56.5 us
  starting transfers between devices: 1.52 us -> 30.2 us
  other arithmetic: 64.3 us -> 35.7 us
  matrix products: 133 us -> 114 us
    reduce_scatter x16 -> x3, waiting for transfers between devices: 555 us -> 99.2 us  [scattered(): lax.psum_scatter(joined, 'fsdp', scatter_dimension=0, tiled=True)]
    all_gather x10 -> x0, blocking collectives: 174 us -> none  [the longest x4 64.7 us: gather_rows(): return lax.all_gather(value, 'tp', axis=0, tiled=True)]
    psum x1 -> x0, waiting for transfers between devices: 127 us -> none  [on_device(): lax.psum((jnp.stack(gain_grads), jnp.stack(shift_grads), jnp.stack(qv_gra...]
    ppermute x0 -> x21, waiting for transfers between devices: none -> 127 us  [the longest x17 109 us: swap(): return lax.ppermute(value, 'tp', [(0, 1), (1, 0)])]
    all_gather x6 -> x3, waiting for transfers between devices: 131 us -> 70.5 us  [gathered(): lax.all_gather(jnp.concatenate(pieces, axis=1), 'fsdp', axis=0, tiled=True)]
    ppermute x0 -> x21, starting transfers between devices: none -> 29.2 us  [the longest x17 25.7 us: swap(): return lax.ppermute(value, 'tp', [(0, 1), (1, 0)])]
    reshape x0 -> x19, local copies, waits for them, and re-layouts: none -> 19.8 us  [the longest x4 6.14 us: attend(): values.reshape(grid_shape)]
    another operation x16 -> x6, local copies, waits for them, and re-layouts: 28.1 us -> 8.52 us  [attend_back(): jnp.stack([query_grad.reshape(flat_shape), key_grad.reshape(flat_shape),...]
  transfers between devices with their start and end apart: 23 -> 27, of which waited for: 20 -> 24; matrix products, arithmetic and copies ran while one was open for 12% -> 26% of each run, Pallas kernels for 0% -> 0%
where the time goes in v1:
time: 555 us; the launch traced here: 549 us
  waiting for transfers between devices  296 us (53%)
  matrix products  114 us (21%)
  local copies, waits for them, and re-layouts  56.5 us (10%)
  other arithmetic  35.7 us (6%)
  starting transfers between devices  30.2 us (5%)
  between operations  16.4 us (3%)
    ppermute x17, waiting for transfers between devices, swap(): return lax.ppermute(value, 'tp', [(0, 1), (1, 0)])  109 us
    reduce_scatter x3, waiting for transfers between devices, scattered(): lax.psum_scatter(joined, 'fsdp', scatter_dimension=0, tiled=True)  99.2 us
    all_gather x3, waiting for transfers between devices, gathered(): lax.all_gather(jnp.concatenate(pieces, axis=1), 'fsdp', axis=0, tiled=True)  70.5 us
    dot_general x12, matrix products, plain(): return jnp.dot(left, right, preferred_element_type=jnp.float32)  44.2 us
    dot_general x16, matrix products, back_product(): lax.dot_general(left, right, (((1,), (1,)), ((), ())), preferred_element_...  32.1 us
    ppermute x17, starting transfers between devices, swap(): return lax.ppermute(value, 'tp', [(0, 1), (1, 0)])  25.7 us
    dot_general x8, matrix products, row_product(): lax.dot_general(left, right, (((0,), (0,)), ((), ())), preferred_element_...  19.8 us
    ppermute x4, waiting for transfers between devices, summed_everywhere(): lax.ppermute(value, 'fsdp', [(place, place ^ step) for place in range(fsd...  18.1 us
  transfers between devices with their start and end apart: 27, of which 24 were waited for; matrix products, arithmetic and copies ran while one was open for 26% of the time, Pallas kernels for 0%

profile of v1, /device:TPU:0, one launch (start us, length us, event | category | flops | bytes accessed | tf_op | source)
XLA Modules:
  0.0 548.9 jit_solution(8241289107425799596)
XLA Ops:
  16.7 10.3 %collective-permute-done = bf16[296,768]{1,0:T(8,128)(2,1)S(1)} collective-permute-done((bf16[296,768]{1,0:T(8,128)(2,1)S(1)}, bf16[296,768]{1,0:T(8,128)(2,1)S(1)}, u32[]{:S(2)}, u32[]{:S(2)}) %collective-permute-start) | collective-permute-done | bytes 454688 | tf_op jit(solution)/shard_map/ppermute | solution.py:42
  27.5 28.4 %all-gather.4.cloned.1.call-done = bf16[768,1536]{1,0:T(8,128)(2,1)} async-done(((bf16[48,1536]{1,0:T(8,128)(2,1)}), bf16[768,1536]{1,0:T(8,128)(2,1)}) %all-gather.4.cloned.1.call-update) | async-done | bytes 2359312 | tf_op jit(solution)/shard_map/all_gather | solution.py:56
  73.9 11.0 %collective-permute-done.1 = bf16[296,768]{1,0:T(8,128)(2,1)S(1)} collective-permute-done((bf16[296,768]{1,0:T(8,128)(2,1)S(1)}, bf16[296,768]{1,0:T(8,128)(2,1)S(1)}, u32[]{:S(2)}, u32[]{:S(2)}) %collective-permute-start.1) | collective-permute-done | bytes 454688 | tf_op jit(solution)/shard_map/ppermute | solution.py:42
  89.3 10.2 %collective-permute-done.2 = bf16[296,768]{1,0:T(8,128)(2,1)S(1)} collective-permute-done((bf16[296,768]{1,0:T(8,128)(2,1)S(1)}, bf16[296,768]{1,0:T(8,128)(2,1)S(1)}, u32[]{:S(2)}, u32[]{:S(2)}) %collective-permute-start.2) | collective-permute-done | bytes 454688 | tf_op jit(solution)/shard_map/ppermute | solution.py:42
  99.5 11.1 %all-gather.6.cloned.1.call-done = bf16[768,3072]{1,0:T(8,128)(2,1)} async-done(((bf16[48,3072]{1,0:T(8,128)(2,1)}), bf16[768,3072]{1,0:T(8,128)(2,1)}) %all-gather.6.cloned.1.call-update) | async-done | bytes 4718608 | tf_op jit(solution)/shard_map/all_gather | solution.py:56
  110.6 8.0 %multiply_convert_fusion.4 = (bf16[296,1536]{1,0:T(8,128)(2,1)S(1)}, f32[296,1536]{1,0:T(8,128)}, f32[296,1536]{1,0:T(8,128)}) fusion(f32[1536]{0:T(1024)S(1)} %dynamic-slice_reduce_fusion.1, bf16[296,768]{1,0:T(8,128)(2,1)S(1)} %collective-permute-done.2, bf16[768,3072]{1,0:T(8,128)(2,1)} %all-gather.6.cloned.1.call-done), kind=kOutput, calls=%fused_computation.87 | convolution fusion | flops 728358912 | bytes 7366656 | tf_op jit(solution)/shard_map/dot_general | solution.py:174
  122.0 6.4 %multiply_convert_fusion.5 = (bf16[296,1536]{1,0:T(8,128)(2,1)S(1)}, f32[296,1536]{1,0:T(8,128)}, f32[296,1536]{1,0:T(8,128)}) fusion(f32[1536]{0:T(1024)S(1)} %dynamic-slice_reduce_fusion.1, bf16[296,768]{1,0:T(8,128)(2,1)S(1)} %add_convert_fusion.6, bf16[768,3072]{1,0:T(8,128)(2,1)S(1)} %copy-done.87), kind=kOutput, calls=%fused_computation.100 | convolution fusion | flops 728358912 | bytes 7368704 | tf_op jit(solution)/shard_map/dot_general | solution.py:174
  128.4 4.7 collective-permute-done.3
  136.4 10.3 %collective-permute-done.4 = bf16[296,768]{1,0:T(8,128)(2,1)S(1)} collective-permute-done((bf16[296,768]{1,0:T(8,128)(2,1)S(1)}, bf16[296,768]{1,0:T(8,128)(2,1)S(1)}, u32[]{:S(2)}, u32[]{:S(2)}) %collective-permute-start.4) | collective-permute-done | bytes 454688 | tf_op jit(solution)/shard_map/ppermute | solution.py:42
  147.0 31.0 %all-gather.8.cloned.1.call-done = bf16[768,4608]{1,0:T(8,128)(2,1)} async-done(((bf16[48,4608]{1,0:T(8,128)(2,1)}), bf16[768,4608]{1,0:T(8,128)(2,1)}) %all-gather.8.cloned.1.call-update) | async-done | bytes 7077904 | tf_op jit(solution)/shard_map/all_gather | solution.py:56
  203.1 11.0 %collective-permute-done.5 = bf16[296,768]{1,0:T(8,128)(2,1)S(1)} collective-permute-done((bf16[296,768]{1,0:T(8,128)(2,1)S(1)}, bf16[296,768]{1,0:T(8,128)(2,1)S(1)}, u32[]{:S(2)}, u32[]{:S(2)}) %collective-permute-start.5) | collective-permute-done | bytes 454688 | tf_op jit(solution)/shard_map/ppermute | solution.py:42
  217.9 6.6 %multiply_convert_fusion.3 = (bf16[296,1536]{1,0:T(8,128)(2,1)S(1)}, f32[296,1536]{1,0:T(8,128)S(1)}, f32[296,1536]{1,0:T(8,128)S(1)}) fusion(f32[1536]{0:T(1024)S(1)} %dynamic-slice_reduce_fusion, bf16[296,768]{1,0:T(8,128)(2,1)S(1)} %add_convert_fusion.4, bf16[768,4608]{1,0:T(8,128)(2,1)} %all-gather.8.cloned.1.call-done), kind=kOutput, calls=%fused_computation.74 | convolution fusion | flops 728358912 | bytes 7366656 | tf_op jit(solution)/shard_map/dot_general | solution.py:174
  224.5 8.3 %collective-permute-done.6 = bf16[296,768]{1,0:T(8,128)(2,1)S(1)} collective-permute-done((bf16[296,768]{1,0:T(8,128)(2,1)S(1)}, bf16[296,768]{1,0:T(8,128)(2,1)S(1)}, u32[]{:S(2)}, u32[]{:S(2)}) %collective-permute-start.6) | collective-permute-done | bytes 454688 | tf_op jit(solution)/shard_map/ppermute | solution.py:42
  232.8 5.4 multiply_convert_fusion.2
  244.7 9.1 %collective-permute-done.9 = bf16[296,768]{1,0:T(8,128)(2,1)S(1)} collective-permute-done((bf16[296,768]{1,0:T(8,128)(2,1)S(1)}, bf16[296,768]{1,0:T(8,128)(2,1)S(1)}, u32[]{:S(2)}, u32[]{:S(2)}) %collective-permute-start.9) | collective-permute-done | bytes 454688 | tf_op jit(solution)/shard_map/ppermute | solution.py:42
  255.5 6.5 %collective-permute-done.7 = bf16[296,768]{1,0:T(8,128)(2,1)S(1)} collective-permute-done((bf16[296,768]{1,0:T(8,128)(2,1)S(1)}, bf16[296,768]{1,0:T(8,128)(2,1)S(1)}, u32[]{:S(2)}, u32[]{:S(2)}) %collective-permute-start.7) | collective-permute-done | bytes 454688 | tf_op jit(solution)/shard_map/ppermute | solution.py:42
  265.6 9.4 %collective-permute-done.10 = bf16[296,768]{1,0:T(8,128)(2,1)S(1)} collective-permute-done((bf16[296,768]{1,0:T(8,128)(2,1)S(1)}, bf16[296,768]{1,0:T(8,128)(2,1)S(1)}, u32[]{:S(2)}, u32[]{:S(2)}) %collective-permute-start.10) | collective-permute-done | bytes 454688 | tf_op jit(solution)/shard_map/ppermute | solution.py:42
  309.9 4.4 collective-permute-done.11
  324.1 4.2 collective-permute-done.12
  328.3 4.1 add_convert_fusion
  340.0 4.3 collective-permute-done.13
  347.9 3.4 convolution_convert_fusion.4
  351.3 3.5 convolution_convert_fusion.5
  378.2 3.4 convolution_convert_fusion.3
  381.6 3.4 pad_maximum_fusion
  388.0 4.0 fusion.108
  396.2 4.4 collective-permute-done.15
  407.9 3.6 collective-permute-done.17
  413.1 7.5 %collective-permute-done.18 = f32[24,768]{1,0:T(8,128)S(1)} collective-permute-done((f32[24,768]{1,0:T(8,128)S(1)}, f32[24,768]{1,0:T(8,128)S(1)}, u32[]{:S(2)}, u32[]{:S(2)}) %collective-permute-start.18) | collective-permute-done | bytes 73760 | tf_op jit(solution)/shard_map/ppermute | solution.py:48
  421.5 5.8 %collective-permute-done.19 = f32[24,768]{1,0:T(8,128)S(1)} collective-permute-done((f32[24,768]{1,0:T(8,128)S(1)}, f32[24,768]{1,0:T(8,128)S(1)}, u32[]{:S(2)}, u32[]{:S(2)}) %collective-permute-start.19) | collective-permute-done | bytes 73760 | tf_op jit(solution)/shard_map/ppermute | solution.py:48
  436.9 7.2 %reduce-scatter.8.cloned.1.call-done = bf16[48,3072]{1,0:T(8,128)(2,1)} async-done(((bf16[768,3072]{1,0:T(8,128)(2,1)}), bf16[48,3072]{1,0:T(8,128)(2,1)}) %reduce-scatter.8.cloned.1.call-update) | async-done | bytes 294928 | tf_op jit(solution)/shard_map/reduce_scatter | solution.py:61
  445.2 92.0 %reduce-scatter.4.cloned.1.call-done = bf16[48,4608]{1,0:T(8,128)(2,1)} async-done(((bf16[768,4608]{1,0:T(8,128)(2,1)}), bf16[48,4608]{1,0:T(8,128)(2,1)}) %reduce-scatter.4.cloned.1.call-update) | async-done | bytes 442384 | tf_op jit(solution)/shard_map/reduce_scatter | solution.py:61
  (464 shorter events, 189.6 us)
Async XLA Ops:
  7.2 48.6 %all-gather.4.cloned.1.call-start = ((), (), s32[]{:S(2)}) async-start(), calls=%async_computation.3 | async-start | bytes 2506752 | tf_op jit(solution)/shard_map/all_gather | solution.py:56
  9.8 100.7 %all-gather.6.cloned.1.call-start = ((), (), s32[]{:S(2)}) async-start(), calls=%async_computation.4 | async-start | bytes 5013504 | tf_op jit(solution)/shard_map/all_gather | solution.py:56
  11.7 166.3 %all-gather.8.cloned.1.call-start = ((), (), s32[]{:S(2)}) async-start(), calls=%async_computation.5 | async-start | bytes 7520256 | tf_op jit(solution)/shard_map/all_gather | solution.py:56
  12.7 422.2 %reduce-scatter.6.cloned.1.call-start = ((), (), s32[]{:S(2)}) async-start(), calls=%async_computation.7 | async-start | bytes 2506752 | tf_op jit(solution)/shard_map/reduce_scatter | solution.py:61
  12.8 74.3 %copy-start.71 = (f32[768]{0:T(1024)}, f32[768]{0:T(1024)S(1)}, u32[]{:S(2)}) copy-start(f32[768]{0:T(1024)S(1)} %get-tuple-element.40) | copy-start | bytes 9220
  13.0 45.6 %copy-start.67 = (f32[296]{0:T(512)}, f32[296]{0:T(512)S(1)}, u32[]{:S(2)}) copy-start(f32[296]{0:T(512)S(1)} %broadcast_multiply_fusion.3) | copy-start | bytes 3556
  13.3 45.3 %copy-start.78 = (f32[296]{0:T(512)}, f32[296]{0:T(512)S(1)}, u32[]{:S(2)}) copy-start(f32[296]{0:T(512)S(1)} %fusion.145) | copy-start | bytes 3556
  13.4 45.3 %copy-start.69 = (f32[296]{0:T(512)}, f32[296]{0:T(512)S(1)}, u32[]{:S(2)}) copy-start(f32[296]{0:T(512)S(1)} %fusion.197) | copy-start | bytes 3556
  13.6 13.5 %collective-permute-start = (bf16[296,768]{1,0:T(8,128)(2,1)S(1)}, bf16[296,768]{1,0:T(8,128)(2,1)S(1)}, u32[]{:S(2)}, u32[]{:S(2)}) collective-permute-start(bf16[296,768]{1,0:T(8,128)(2,1)S(1)} %fusion.143), channel_id=1, source_target_pairs={{0,1},{1,0},{2,3},{3,2},{4,5},{5,4},{6,7},{7,6},{8,9},{9,8},{10,11... | collective-permute-start | bytes 1363976 | tf_op jit(solution)/shard_map/ppermute | solution.py:42
  72.3 12.6 %collective-permute-start.1 = (bf16[296,768]{1,0:T(8,128)(2,1)S(1)}, bf16[296,768]{1,0:T(8,128)(2,1)S(1)}, u32[]{:S(2)}, u32[]{:S(2)}) collective-permute-start(bf16[296,768]{1,0:T(8,128)(2,1)S(1)} %convolution_convert_fusion.9), channel_id=1, source_target_pairs={{0,1},{1,0},{2,3},{3,2},{4,5},{5,4},{6,7},{7,6},{8,9},{9,8},{10,11... | collective-permute-start | bytes 1363976 | tf_op jit(solution)/shard_map/ppermute | solution.py:42
  87.7 11.8 %collective-permute-start.2 = (bf16[296,768]{1,0:T(8,128)(2,1)S(1)}, bf16[296,768]{1,0:T(8,128)(2,1)S(1)}, u32[]{:S(2)}, u32[]{:S(2)}) collective-permute-start(bf16[296,768]{1,0:T(8,128)(2,1)S(1)} %add_convert_fusion.6), channel_id=1, source_target_pairs={{0,1},{1,0},{2,3},{3,2},{4,5},{5,4},{6,7},{7,6},{8,9},{9,8},{10,11... | collective-permute-start | bytes 1363976 | tf_op jit(solution)/shard_map/ppermute | solution.py:42
  120.5 12.6 %collective-permute-start.3 = (bf16[296,768]{1,0:T(8,128)(2,1)S(1)}, bf16[296,768]{1,0:T(8,128)(2,1)S(1)}, u32[]{:S(2)}, u32[]{:S(2)}) collective-permute-start(bf16[296,768]{1,0:T(8,128)(2,1)S(1)} %fusion.117), channel_id=1, source_target_pairs={{0,1},{1,0},{2,3},{3,2},{4,5},{5,4},{6,7},{7,6},{8,9},{9,8},{10,11... | collective-permute-start | bytes 1363976 | tf_op jit(solution)/shard_map/ppermute | solution.py:42
  134.7 11.9 %collective-permute-start.4 = (bf16[296,768]{1,0:T(8,128)(2,1)S(1)}, bf16[296,768]{1,0:T(8,128)(2,1)S(1)}, u32[]{:S(2)}, u32[]{:S(2)}) collective-permute-start(bf16[296,768]{1,0:T(8,128)(2,1)S(1)} %add_convert_fusion.5), channel_id=1, source_target_pairs={{0,1},{1,0},{2,3},{3,2},{4,5},{5,4},{6,7},{7,6},{8,9},{9,8},{10,11... | collective-permute-start | bytes 1363976 | tf_op jit(solution)/shard_map/ppermute | solution.py:42
  200.7 13.4 %collective-permute-start.5 = (bf16[296,768]{1,0:T(8,128)(2,1)S(1)}, bf16[296,768]{1,0:T(8,128)(2,1)S(1)}, u32[]{:S(2)}, u32[]{:S(2)}) collective-permute-start(bf16[296,768]{1,0:T(8,128)(2,1)S(1)} %convolution_convert_fusion.8), channel_id=1, source_target_pairs={{0,1},{1,0},{2,3},{3,2},{4,5},{5,4},{6,7},{7,6},{8,9},{9,8},{10,11... | collective-permute-start | bytes 1363976 | tf_op jit(solution)/shard_map/ppermute | solution.py:42
  202.4 39.6 %copy-start.48 = (bf16[296,768]{1,0:T(8,128)(2,1)}, bf16[296,768]{1,0:T(8,128)(2,1)S(1)}, u32[]{:S(2)}) copy-start(bf16[296,768]{1,0:T(8,128)(2,1)S(1)} %get-tuple-element.52) | copy-start | bytes 1363972
  202.4 35.8 %collective-permute-start.8 = (bf16[296,768]{1,0:T(8,128)(2,1)S(1)}, bf16[296,768]{1,0:T(8,128)(2,1)S(1)}, u32[]{:S(2)}, u32[]{:S(2)}) collective-permute-start(bf16[296,768]{1,0:T(8,128)(2,1)S(1)} %get-tuple-element.52), channel_id=1, source_target_pairs={{0,1},{1,0},{2,3},{3,2},{4,5},{5,4},{6,7},{7,6},{8,9},{9,8},{10,11... | collective-permute-start | bytes 1363976 | tf_op jit(solution)/shard_map/ppermute | solution.py:42
  216.4 16.4 %collective-permute-start.6 = (bf16[296,768]{1,0:T(8,128)(2,1)S(1)}, bf16[296,768]{1,0:T(8,128)(2,1)S(1)}, u32[]{:S(2)}, u32[]{:S(2)}) collective-permute-start(bf16[296,768]{1,0:T(8,128)(2,1)S(1)} %add_convert_fusion.4), channel_id=1, source_target_pairs={{0,1},{1,0},{2,3},{3,2},{4,5},{5,4},{6,7},{7,6},{8,9},{9,8},{10,11... | collective-permute-start | bytes 1363976 | tf_op jit(solution)/shard_map/ppermute | solution.py:42
  240.4 13.4 %collective-permute-start.9 = (bf16[296,768]{1,0:T(8,128)(2,1)S(1)}, bf16[296,768]{1,0:T(8,128)(2,1)S(1)}, u32[]{:S(2)}, u32[]{:S(2)}) collective-permute-start(bf16[296,768]{1,0:T(8,128)(2,1)S(1)} %fusion.120), channel_id=1, source_target_pairs={{0,1},{1,0},{2,3},{3,2},{4,5},{5,4},{6,7},{7,6},{8,9},{9,8},{10,11... | collective-permute-start | bytes 1363976 | tf_op jit(solution)/shard_map/ppermute | solution.py:42
  244.1 17.8 %collective-permute-start.7 = (bf16[296,768]{1,0:T(8,128)(2,1)S(1)}, bf16[296,768]{1,0:T(8,128)(2,1)S(1)}, u32[]{:S(2)}, u32[]{:S(2)}) collective-permute-start(bf16[296,768]{1,0:T(8,128)(2,1)S(1)} %fusion.123), channel_id=1, source_target_pairs={{0,1},{1,0},{2,3},{3,2},{4,5},{5,4},{6,7},{7,6},{8,9},{9,8},{10,11... | collective-permute-start | bytes 1363976 | tf_op jit(solution)/shard_map/ppermute | solution.py:42
  264.1 10.9 %collective-permute-start.10 = (bf16[296,768]{1,0:T(8,128)(2,1)S(1)}, bf16[296,768]{1,0:T(8,128)(2,1)S(1)}, u32[]{:S(2)}, u32[]{:S(2)}) collective-permute-start(bf16[296,768]{1,0:T(8,128)(2,1)S(1)} %get-tuple-element.54), channel_id=1, source_target_pairs={{0,1},{1,0},{2,3},{3,2},{4,5},{5,4},{6,7},{7,6},{8,9},{9,8},{10,11... | collective-permute-start | bytes 1363976 | tf_op jit(solution)/shard_map/ppermute | solution.py:42
  300.9 143.2 %reduce-scatter.8.cloned.1.call-start = ((), (), s32[]{:S(2)}) async-start(), calls=%async_computation.8 | async-start | bytes 5013504 | tf_op jit(solution)/shard_map/reduce_scatter | solution.py:61
  304.3 10.1 %collective-permute-start.11 = (bf16[296,768]{1,0:T(8,128)(2,1)S(1)}, bf16[296,768]{1,0:T(8,128)(2,1)S(1)}, u32[]{:S(2)}, u32[]{:S(2)}) collective-permute-start(bf16[296,768]{1,0:T(8,128)(2,1)S(1)} %fusion.111), channel_id=1, source_target_pairs={{0,1},{1,0},{2,3},{3,2},{4,5},{5,4},{6,7},{7,6},{8,9},{9,8},{10,11... | collective-permute-start | bytes 1363976 | tf_op jit(solution)/shard_map/ppermute | solution.py:42
  319.1 9.2 %collective-permute-start.12 = (bf16[296,768]{1,0:T(8,128)(2,1)S(1)}, bf16[296,768]{1,0:T(8,128)(2,1)S(1)}, u32[]{:S(2)}, u32[]{:S(2)}) collective-permute-start(bf16[296,768]{1,0:T(8,128)(2,1)S(1)} %get-tuple-element.56), channel_id=1, source_target_pairs={{0,1},{1,0},{2,3},{3,2},{4,5},{5,4},{6,7},{7,6},{8,9},{9,8},{10,11... | collective-permute-start | bytes 1363976 | tf_op jit(solution)/shard_map/ppermute | solution.py:42
  323.4 213.7 %reduce-scatter.4.cloned.1.call-start = ((), (), s32[]{:S(2)}) async-start(), calls=%async_computation.6 | async-start | bytes 7520256 | tf_op jit(solution)/shard_map/reduce_scatter | solution.py:61
  335.4 8.9 %collective-permute-start.13 = (bf16[296,768]{1,0:T(8,128)(2,1)S(1)}, bf16[296,768]{1,0:T(8,128)(2,1)S(1)}, u32[]{:S(2)}, u32[]{:S(2)}) collective-permute-start(bf16[296,768]{1,0:T(8,128)(2,1)S(1)} %fusion.114), channel_id=1, source_target_pairs={{0,1},{1,0},{2,3},{3,2},{4,5},{5,4},{6,7},{7,6},{8,9},{9,8},{10,11... | collective-permute-start | bytes 1363976 | tf_op jit(solution)/shard_map/ppermute | solution.py:42
  346.4 8.5 %collective-permute-start.14 = (bf16[296,768]{1,0:T(8,128)(2,1)S(1)}, bf16[296,768]{1,0:T(8,128)(2,1)S(1)}, u32[]{:S(2)}, u32[]{:S(2)}) collective-permute-start(bf16[296,768]{1,0:T(8,128)(2,1)S(1)} %get-tuple-element.59), channel_id=1, source_target_pairs={{0,1},{1,0},{2,3},{3,2},{4,5},{5,4},{6,7},{7,6},{8,9},{9,8},{10,11... | collective-permute-start | bytes 1363976 | tf_op jit(solution)/shard_map/ppermute | solution.py:42
  392.0 8.6 %collective-permute-start.15 = (bf16[296,768]{1,0:T(8,128)(2,1)}, bf16[296,768]{1,0:T(8,128)(2,1)S(1)}, u32[]{:S(2)}, u32[]{:S(2)}) collective-permute-start(bf16[296,768]{1,0:T(8,128)(2,1)} %fusion.108), channel_id=1, source_target_pairs={{0,1},{1,0},{2,3},{3,2},{4,5},{5,4},{6,7},{7,6},{8,9},{9,8},{10,11... | collective-permute-start | bytes 1363976 | tf_op jit(solution)/shard_map/ppermute | solution.py:42
  405.6 1.3 collective-permute-start.16
  406.9 4.6 collective-permute-start.17
  411.6 9.0 %collective-permute-start.18 = (f32[24,768]{1,0:T(8,128)S(1)}, f32[24,768]{1,0:T(8,128)S(1)}, u32[]{:S(2)}, u32[]{:S(2)}) collective-permute-start(f32[24,768]{1,0:T(8,128)S(1)} %add.396), channel_id=1, source_target_pairs={{0,8},{2,10},{4,12},{6,14},{8,0},{10,2},{12,4},{14,6},{16,24},{18,... | collective-permute-start | bytes 221192 | tf_op jit(solution)/shard_map/ppermute | solution.py:48
  420.6 6.8 %collective-permute-start.19 = (f32[24,768]{1,0:T(8,128)S(1)}, f32[24,768]{1,0:T(8,128)S(1)}, u32[]{:S(2)}, u32[]{:S(2)}) collective-permute-start(f32[24,768]{1,0:T(8,128)S(1)} %add.397), channel_id=1, source_target_pairs={{0,16},{2,18},{4,20},{6,22},{8,24},{10,26},{12,28},{14,30},{16,0},... | collective-permute-start | bytes 221192 | tf_op jit(solution)/shard_map/ppermute | solution.py:48
  427.4 4.4 collective-permute-start.20
  (105 other events, 747.5 us)
Sparse Core Ops, SparseCore 0:
  10.8 44.9 all-gather.3
  58.7 51.8 all-gather.5
  113.4 64.5 all-gather.7
  301.0 61.9 reduce-scatter.5
  366.7 77.3 reduce-scatter.7
  448.0 89.1 reduce-scatter.3

commit v2 on v1

v2 whole, which is shorter than its diff:
```python
import math

import jax
import jax.numpy as jnp
from jax import lax
from jax.experimental import pallas as pl
from jax.experimental.pallas import tpu as pltpu
from jax.sharding import PartitionSpec as P

D = 768
HEADS = 12
FF = 3072
SEQ = 197
LAYERS = 2
IMG_DEV = 3


def norm_rows(value, gain_vector, shift_vector):
    row_mean = jnp.mean(value, axis=-1, keepdims=True)
    centred = value - row_mean
    row_var = jnp.mean(centred * centred, axis=-1, keepdims=True)
    return centred * lax.rsqrt(row_var + 1e-06) * gain_vector + shift_vector


def row_product(left, right):
    return lax.dot_general(
        left, right, (((0,), (0,)), ((), ())), preferred_element_type=jnp.float32
    )


def halves(own, other, first):
    return jnp.concatenate(
        [jnp.where(first, own, other), jnp.where(first, other, own)], axis=0
    )


def swap(value):
    return lax.ppermute(value, "tp", [(0, 1), (1, 0)])


def summed_everywhere(value, fsdp_count):
    step = 1
    while step < fsdp_count:
        value = value + lax.ppermute(
            value, "fsdp", [(place, place ^ step) for place in range(fsdp_count)]
        )
        step *= 2
    return value + swap(value)


def gathered(pieces):
    return lax.all_gather(jnp.concatenate(pieces, axis=1), "fsdp", axis=0, tiled=True)


def scattered(joined):
    return lax.psum_scatter(joined, "fsdp", scatter_dimension=0, tiled=True).astype(jnp.float32)


WINDOW = 208
WINDOW_STEP = 192
LANES = 128
FAR_BELOW = -1e30


def turned_product(left, right):
    return lax.dot_general(
        left, right, (((1,), (1,)), ((), ())), preferred_element_type=jnp.float32
    )


def plain_product(left, right):
    return jnp.dot(left, right, preferred_element_type=jnp.float32)


def window_masks(image):
    low = (SEQ - WINDOW_STEP) * image
    high = low + SEQ
    rows = lax.broadcasted_iota(jnp.int32, (WINDOW, 1), 0)
    columns = lax.broadcasted_iota(jnp.int32, (1, WINDOW), 1)
    return (rows >= low) & (rows < high), (columns >= low) & (columns < high)


def window_chances(query_head, key_pair, row_live, column_live, scale):
    scores = jnp.where(column_live, turned_product(query_head, key_pair) * scale, FAR_BELOW)
    expanded = jnp.exp(scores - jnp.max(scores, axis=-1, keepdims=True))
    total = jnp.sum(expanded, axis=-1, keepdims=True)
    return jnp.where(row_live, expanded / total, 0.0)


def attend_kernel(
    place_ref,
    hidden_ref,
    weight_ref,
    turned_ref,
    bias_ref,
    qkv_ref,
    mixed_ref,
    sent_ref,
    kept_ref,
    mixed_wide,
):
    width = mixed_ref.shape[1]
    row_count = sent_ref.shape[0]
    scale = (D // HEADS) ** (-0.5)
    hidden = hidden_ref[...]
    for part in range(3):
        span = pl.ds(part * width, width)
        product = plain_product(hidden, weight_ref[:, span])
        if part != 1:
            product = product + bias_ref[pl.ds(part // 2, 1), :]
        qkv_ref[:, span] = product.astype(jnp.bfloat16)
    mixed_wide[...] = jnp.zeros_like(mixed_wide)
    lane_low = lax.broadcasted_iota(jnp.int32, (1, LANES), 1) < D // HEADS

    def one_image(image, carry):
        window = pl.ds(pl.multiple_of(image * WINDOW_STEP, 16), WINDOW)
        row_live, column_live = window_masks(image)
        for pair in range(width // LANES):
            query_pair = qkv_ref[window, pl.ds(pair * LANES, LANES)]
            key_pair = qkv_ref[window, pl.ds(width + pair * LANES, LANES)]
            value_pair = qkv_ref[window, pl.ds(2 * width + pair * LANES, LANES)]
            sides = []
            for lane_mask in (lane_low, ~lane_low):
                chances = window_chances(
                    jnp.where(lane_mask, query_pair, jnp.zeros_like(query_pair)),
                    key_pair,
                    row_live,
                    column_live,
                    scale,
                )
                sides.append(plain_product(chances.astype(jnp.bfloat16), value_pair))
            mixed_wide[window, pl.ds(pair * LANES, LANES)] += jnp.where(
                lane_low, sides[0], sides[1]
            )
        return carry

    lax.fori_loop(0, IMG_DEV, one_image, 0)
    mixed_ref[...] = mixed_wide[...].astype(jnp.bfloat16)
    turned = turned_ref[...]
    place = place_ref[0]
    other = pl.ds(pl.multiple_of((1 - place) * row_count, 8), row_count)
    own = pl.ds(pl.multiple_of(place * row_count, 8), row_count)
    sent_ref[...] = turned_product(mixed_wide[other, :].astype(jnp.bfloat16), turned).astype(
        jnp.bfloat16
    )
    kept_ref[...] = turned_product(mixed_wide[own, :].astype(jnp.bfloat16), turned)


def attend_back_kernel(
    place_ref,
    branch_ref,
    qkv_ref,
    weight_ref,
    turned_ref,
    stacked_ref,
    sent_ref,
    kept_ref,
    sums_ref,
    mixed_grad,
    wide,
):
    width = mixed_grad.shape[1]
    row_count = sent_ref.shape[0]
    scale = (D // HEADS) ** (-0.5)
    mixed_grad[...] = plain_product(branch_ref[...], turned_ref[...]).astype(jnp.bfloat16)
    wide[...] = jnp.zeros_like(wide)
    lane_low = lax.broadcasted_iota(jnp.int32, (1, LANES), 1) < D // HEADS

    def one_image(image, carry):
        window = pl.ds(pl.multiple_of(image * WINDOW_STEP, 16), WINDOW)
        row_live, column_live = window_masks(image)
        for pair in range(width // LANES):
            query_pair = qkv_ref[window, pl.ds(pair * LANES, LANES)]
            key_pair = qkv_ref[window, pl.ds(width + pair * LANES, LANES)]
            value_pair = qkv_ref[window, pl.ds(2 * width + pair * LANES, LANES)]
            grad_pair = mixed_grad[window, pl.ds(pair * LANES, LANES)]
            sides = []
            for lane_mask in (lane_low, ~lane_low):
                chances = window_chances(
                    jnp.where(lane_mask, query_pair, jnp.zeros_like(query_pair)),
                    key_pair,
                    row_live,
                    column_live,
                    scale,
                )
                weight_grad = turned_product(
                    jnp.where(lane_mask, grad_pair, jnp.zeros_like(grad_pair)), value_pair
                )
                row_sum = jnp.sum(weight_grad * chances, axis=-1, keepdims=True)
                score_grad = (chances * (weight_grad - row_sum)).astype(jnp.bfloat16)
                sides.append(
                    (
                        plain_product(score_grad, key_pair) * scale,
                        row_product(score_grad, query_pair) * scale,
                        row_product(chances.astype(jnp.bfloat16), grad_pair),
                    )
                )
            for part in range(3):
                wide[window, pl.ds(part * width + pair * LANES, LANES)] += jnp.where(
                    lane_low, sides[0][part], sides[1][part]
                )
        return carry

    lax.fori_loop(0, IMG_DEV, one_image, 0)
    stacked = wide[...].astype(jnp.bfloat16)
    stacked_ref[...] = stacked
    sums_ref[...] = jnp.sum(stacked.astype(jnp.float32), axis=0, keepdims=True)
    place = place_ref[0]
    other = pl.ds(pl.multiple_of((1 - place) * row_count, 8), row_count)
    own = pl.ds(pl.multiple_of(place * row_count, 8), row_count)
    weight = weight_ref[...]
    sent_ref[...] = turned_product(wide[other, :].astype(jnp.bfloat16), weight).astype(jnp.bfloat16)
    kept_ref[...] = turned_product(wide[own, :].astype(jnp.bfloat16), weight)


def attend_grads_kernel(hidden_ref, stacked_ref, branch_ref, mixed_ref, grad_ref):
    cut = stacked_ref.shape[1]
    grad_ref[:, :cut] = row_product(hidden_ref[...], stacked_ref[...]).astype(jnp.bfloat16)
    grad_ref[:, cut:] = row_product(branch_ref[...], mixed_ref[...]).astype(jnp.bfloat16)


def mlp_kernel(hidden_ref, up_ref, turned_ref, bias_ref, act_ref, slope_ref, partial_ref):
    pre = plain_product(hidden_ref[...], up_ref[...]) + bias_ref[...]
    normal = 0.5 * (1.0 + lax.erf(pre * (0.5**0.5)))
    density = jnp.exp(-0.5 * pre * pre) * (0.5 / math.pi) ** 0.5
    active = (pre * normal).astype(jnp.bfloat16)
    act_ref[...] = active
    slope_ref[...] = (normal + pre * density).astype(jnp.bfloat16)
    partial_ref[...] = turned_product(active, turned_ref[...]).astype(partial_ref.dtype)


def mlp_back_kernel(branch_ref, slope_ref, turned_ref, up_ref, pre_ref, partial_ref, sums_ref):
    act_grad = plain_product(branch_ref[...], turned_ref[...])
    pre_grad = (act_grad * slope_ref[...].astype(jnp.float32)).astype(jnp.bfloat16)
    pre_ref[...] = pre_grad
    partial_ref[...] = turned_product(pre_grad, up_ref[...]).astype(partial_ref.dtype)
    sums_ref[...] = jnp.sum(pre_grad.astype(jnp.float32), axis=0, keepdims=True)


def mlp_grads_kernel(
    hidden_own, hidden_other, pre_own, pre_other, branch_own, branch_other, act_own, act_other, grad_ref
):
    cut = pre_own.shape[1]
    grad_ref[:, :cut] = (
        row_product(hidden_own[...], pre_own[...]) + row_product(hidden_other[...], pre_other[...])
    ).astype(jnp.bfloat16)
    grad_ref[:, cut:] = (
        row_product(branch_own[...], act_own[...]) + row_product(branch_other[...], act_other[...])
    ).astype(jnp.bfloat16)


ROOM = 60 * 1024 * 1024


def columns(array, width, place):
    return array, pl.BlockSpec((array.shape[0], width), lambda step: (0, place))


def whole(array):
    return array, pl.BlockSpec(array.shape, lambda step: (0,) * array.ndim)


def scalar(array):
    return array, pl.BlockSpec(memory_space=pltpu.SMEM)


def run_kernel(kernel, operands, results, scratch=(), name=None, flops=0):
    outs = [jax.ShapeDtypeStruct(shape, dtype) for shape, dtype in results]
    return pl.pallas_call(
        kernel,
        grid=(1,),
        in_specs=[spec for array, spec in operands],
        out_specs=[pl.BlockSpec(shape, lambda step, rank=len(shape): (0,) * rank) for shape, dtype in results],
        out_shape=outs,
        scratch_shapes=list(scratch),
        compiler_params=pltpu.CompilerParams(vmem_limit_bytes=ROOM),
        cost_estimate=pl.CostEstimate(
            flops=flops,
            transcendentals=0,
            bytes_accessed=sum(math.prod(out.shape) * out.dtype.itemsize for out in outs),
        ),
        name=name,
    )(*[array for array, spec in operands])


def on_device(
    tokens,
    qkv_weight,
    out_weight,
    up_weight,
    down_weight,
    norm_gain,
    norm_shift,
    qv_bias,
    out_bias,
    up_bias,
    cotangent,
):
    tp_index = lax.axis_index("tp")
    tp_count = lax.axis_size("tp")
    fsdp_count = lax.axis_size("fsdp")
    row_count = tokens.shape[0]
    local_width = qkv_weight.shape[3]
    inner_width = up_weight.shape[2]
    piece_rows = qkv_weight.shape[1]
    all_rows = IMG_DEV * SEQ
    slot_rows = row_count * tp_count
    first = tp_index == 0
    live = (tp_index * row_count + jnp.arange(row_count) < all_rows)[:, None]
    cut_qkv = 3 * local_width
    cut_out = cut_qkv + local_width

    place = jnp.reshape(tp_index, (1,)).astype(jnp.int32)
    bf16 = jnp.bfloat16
    f32 = jnp.float32

    def attn_pieces(layer_index):
        return [
            qkv_weight[layer_index].reshape(piece_rows, cut_qkv),
            out_weight[layer_index].T,
        ]

    def mlp_pieces(layer_index):
        return [up_weight[layer_index], down_weight[layer_index].T]

    attn_zero = gathered(attn_pieces(0))
    mlp_zero = gathered(mlp_pieces(0))
    full_one = gathered(attn_pieces(1) + mlp_pieces(1))
    sources = [
        (attn_zero, mlp_zero, 0, 1),
        (full_one, full_one, 1, 2),
    ]

    stream = tokens.astype(jnp.float32)
    saved_values = []
    for layer_index in range(LAYERS):
        attn_full, mlp_full, up_place, down_place = sources[layer_index]
        qkv_side = columns(attn_full, cut_qkv, 0)
        out_side = columns(attn_full, local_width, 3)
        up_side = columns(mlp_full, inner_width, up_place)
        down_side = columns(mlp_full, inner_width, down_place)
        local_qv = lax.dynamic_slice_in_dim(
            qv_bias[layer_index], tp_index * local_width, local_width, 1
        )
        local_up = lax.dynamic_slice_in_dim(
            up_bias[layer_index], tp_index * inner_width, inner_width, 0
        )[None]
        layer_input = stream
        own_hidden = norm_rows(
            stream, norm_gain[layer_index, 0], norm_shift[layer_index, 0]
        ).astype(bf16)
        hidden = halves(own_hidden, swap(own_hidden), first)
        qkv, mixed, sent, kept = run_kernel(
            attend_kernel,
            [scalar(place), whole(hidden), qkv_side, out_side, whole(local_qv)],
            [
                ((slot_rows, cut_qkv), bf16),
                ((slot_rows, local_width), bf16),
                ((row_count, D), bf16),
                ((row_count, D), f32),
            ],
            [pltpu.VMEM((slot_rows, local_width), f32)],
            name="attend",
        )
        stream = stream + (kept + swap(sent).astype(f32)) + out_bias[layer_index, 0]
        middle = stream
        hidden_own = norm_rows(
            stream, norm_gain[layer_index, 1], norm_shift[layer_index, 1]
        ).astype(bf16)
        hidden_other = swap(hidden_own)

        def mlp_half(hidden_half, kind):
            return run_kernel(
                mlp_kernel,
                [whole(hidden_half), up_side, down_side, whole(local_up)],
                [
                    ((row_count, inner_width), bf16),
                    ((row_count, inner_width), bf16),
                    ((row_count, D), kind),
                ],
                name="mlp",
            )

        act_own, slope_own, kept = mlp_half(hidden_own, f32)
        act_other, slope_other, sent = mlp_half(hidden_other, bf16)
        stream = stream + (kept + swap(sent).astype(f32)) + out_bias[layer_index, 1]
        saved_values.append(
            (
                layer_input,
                middle,
                hidden,
                qkv,
                mixed,
                hidden_own,
                hidden_other,
                slope_own,
                slope_other,
                act_own,
                act_other,
                (qkv_side, out_side, up_side, down_side),
            )
        )
    activations = jnp.where(live, stream, 0.0).astype(jnp.bfloat16)
    grad = jnp.where(live, cotangent.astype(jnp.float32), 0.0)
    owned = []
    gain_grads = [None] * LAYERS
    shift_grads = [None] * LAYERS
    qv_grads = [None] * LAYERS
    out_bias_grads = [None] * LAYERS
    up_bias_grads = [None] * LAYERS
    for layer_index in reversed(range(LAYERS)):
        (
            layer_input,
            middle,
            hidden,
            qkv,
            mixed,
            hidden_own,
            hidden_other,
            slope_own,
            slope_other,
            act_own,
            act_other,
            (qkv_side, out_side, up_side, down_side),
        ) = saved_values[layer_index]
        branch_own = grad.astype(bf16)
        down_bias_grad = jnp.sum(branch_own.astype(f32), axis=0)
        branch_other = swap(branch_own)

        def mlp_half_back(branch, slope, kind):
            return run_kernel(
                mlp_back_kernel,
                [whole(branch), whole(slope), down_side, up_side],
                [((row_count, inner_width), bf16), ((row_count, D), kind), ((1, inner_width), f32)],
                name="mlp_back",
            )

        pre_own, kept, up_sums_own = mlp_half_back(branch_own, slope_own, f32)
        pre_other, sent, up_sums_other = mlp_half_back(branch_other, slope_other, bf16)
        norm_grad = kept + swap(sent).astype(f32)
        up_vector_grad = (up_sums_own + up_sums_other)[0]
        (mlp_grad,) = run_kernel(
            mlp_grads_kernel,
            [
                whole(part)
                for part in (
                    hidden_own,
                    hidden_other,
                    pre_own,
                    pre_other,
                    branch_own,
                    branch_other,
                    act_own,
                    act_other,
                )
            ],
            [((D, 2 * inner_width), bf16)],
            name="mlp_grads",
        )
        norm_back = jax.vjp(
            norm_rows, middle, norm_gain[layer_index, 1], norm_shift[layer_index, 1]
        )[1]
        middle_grad, gain_two, shift_two = norm_back(norm_grad)
        grad = grad + middle_grad
        branch_own = grad.astype(bf16)
        attn_bias_grad = jnp.sum(branch_own.astype(f32), axis=0)
        branch_full = halves(branch_own, swap(branch_own), first)
        stacked, sent, kept, stacked_sums = run_kernel(
            attend_back_kernel,
            [scalar(place), whole(branch_full), whole(qkv), qkv_side, out_side],
            [
                ((slot_rows, cut_qkv), bf16),
                ((row_count, D), bf16),
                ((row_count, D), f32),
                ((1, cut_qkv), f32),
            ],
            [pltpu.VMEM((slot_rows, local_width), bf16), pltpu.VMEM((slot_rows, cut_qkv), f32)],
            name="attend_back",
        )
        norm_grad = kept + swap(sent).astype(f32)
        stacked_sums = stacked_sums.reshape(3, local_width)
        (attn_grad,) = run_kernel(
            attend_grads_kernel,
            [whole(hidden), whole(stacked), whole(branch_full), whole(mixed)],
            [((D, cut_out), bf16)],
            name="attend_grads",
        )
        norm_back = jax.vjp(
            norm_rows, layer_input, norm_gain[layer_index, 0], norm_shift[layer_index, 0]
        )[1]
        input_part, gain_one, shift_one = norm_back(norm_grad)
        grad = grad + input_part
        if layer_index:
            owned.append((scattered(mlp_grad), scattered(attn_grad)))
        else:
            joined = scattered(jnp.concatenate([mlp_grad, attn_grad], axis=1))
            owned.append((joined[:, : 2 * inner_width], joined[:, 2 * inner_width :]))
        gain_grads[layer_index] = jnp.stack([gain_one, gain_two])
        shift_grads[layer_index] = jnp.stack([shift_one, shift_two])
        qv_local = jnp.stack([stacked_sums[0], stacked_sums[2]])
        qv_grads[layer_index] = lax.dynamic_update_slice_in_dim(
            jnp.zeros((2, D), jnp.float32), qv_local, tp_index * local_width, 1
        )
        out_bias_grads[layer_index] = jnp.stack([attn_bias_grad, down_bias_grad])
        up_bias_grads[layer_index] = lax.dynamic_update_slice_in_dim(
            jnp.zeros((FF,), jnp.float32), up_vector_grad, tp_index * inner_width, 0
        ).reshape(FF // D, D)
    small = jnp.concatenate(
        gain_grads + shift_grads + qv_grads + out_bias_grads + up_bias_grads, axis=0
    )
    small = summed_everywhere(small, fsdp_count)
    pair = 2 * LAYERS
    small_totals = [small[pair * k : pair * (k + 1)].reshape(LAYERS, 2, D) for k in range(4)]
    up_totals = small[4 * pair :].reshape(LAYERS, FF)
    owned = owned[::-1]
    up_all = jnp.stack([mlp[:, :inner_width] for mlp, attn in owned])
    down_all = jnp.stack([mlp[:, inner_width:].T for mlp, attn in owned])
    qkv_all = jnp.stack(
        [attn[:, :cut_qkv].reshape(piece_rows, 3, local_width) for mlp, attn in owned]
    )
    out_all = jnp.stack([attn[:, cut_qkv:].T for mlp, attn in owned])
    input_grad = jnp.where(live, grad, 0.0)
    return (
        activations,
        input_grad,
        qkv_all,
        out_all,
        up_all,
        down_all,
        small_totals[0],
        small_totals[1],
        small_totals[2],
        small_totals[3],
        up_totals,
    )


def solution(mesh):
    return jax.shard_map(
        on_device,
        mesh=mesh,
        in_specs=(
            P(("fsdp", "tp"), None),
            P(None, "fsdp", None, "tp"),
            P(None, "tp", "fsdp"),
            P(None, "fsdp", "tp"),
            P(None, "tp", "fsdp"),
            P(),
            P(),
            P(),
            P(),
            P(),
            P(("fsdp", "tp"), None),
        ),
        out_specs=(
            P(("fsdp", "tp"), None),
            P(("fsdp", "tp"), None),
            P(None, "fsdp", None, "tp"),
            P(None, "tp", "fsdp"),
            P(None, "fsdp", "tp"),
            P(None, "tp", "fsdp"),
            P(),
            P(),
            P(),
            P(),
            P(),
        ),
        check_vma=False,
    )
```

time: 555 us -> 545 us (0.982)
  Pallas kernels: 0 us -> 125 us
  matrix products: 114 us -> 0 us
  local copies, waits for them, and re-layouts: 56.5 us -> 15 us
  waiting for transfers between devices: 296 us -> 312 us
    pallas_call x0 -> x16, Pallas kernels: none -> 125 us  [run_kernel(): pl.pallas_call(kernel, grid=(1,), in_specs=[spec for array, spec in opera...]
    dot_general x48 -> x0, matrix products: 114 us -> none  [the longest x12 44.2 us: plain(): return jnp.dot(left, right, preferred_element_type=jnp.float32)]
    reshape x16 -> x0, local copies, waits for them, and re-layouts: 22.4 us -> none  [the longest x4 6.14 us: attend(): values.reshape(grid_shape)]
    convert_element_type x10 -> x0, local copies, waits for them, and re-layouts: 9.06 us -> none  [the longest x4 4.03 us: attend(): mixed.reshape(images * SEQ, local_heads * head_dim).astype(jnp.bfloat16)]
    all_gather x3, waiting for transfers between devices: 70.5 us -> 79.2 us  [gathered(): lax.all_gather(jnp.concatenate(pieces, axis=1), 'fsdp', axis=0, tiled=True)]
    another operation x10 -> x4, local copies, waits for them, and re-layouts: 8.53 us -> 0.01 us  [the longest x6 8.52 us: attend_back(): jnp.stack([query_grad.reshape(flat_shape), key_grad.reshape(flat_shape),...]
    reduce_sum x10 -> x4, other arithmetic: 6.82 us -> 0.96 us  [the longest x2 0.5 us: on_device(): down_bias_grad = jnp.sum(branch_own.astype(f32), axis=0)]
  transfers between devices with their start and end apart: 27 -> 27, of which waited for: 24 -> 25; matrix products, arithmetic and copies ran while one was open for 26% -> 7% of each run, Pallas kernels for 0% -> 16%
where the time goes in v2:
time: 545 us; the launch traced here: 537 us
  waiting for transfers between devices  312 us (57%)
  Pallas kernels  125 us (23%)
  other arithmetic  39.8 us (7%)
  starting transfers between devices  29.6 us (5%)
  between operations  15.2 us (3%)
  local copies, waits for them, and re-layouts  15 us (3%)
    pallas_call x16, Pallas kernels, run_kernel(): pl.pallas_call(kernel, grid=(1,), in_specs=[spec for array, spec in opera...  125 us
    ppermute x17, waiting for transfers between devices, swap(): return lax.ppermute(value, 'tp', [(0, 1), (1, 0)])  113 us
    reduce_scatter x3, waiting for transfers between devices, scattered(): lax.psum_scatter(joined, 'fsdp', scatter_dimension=0, tiled=True)  103 us
    all_gather x3, waiting for transfers between devices, gathered(): lax.all_gather(jnp.concatenate(pieces, axis=1), 'fsdp', axis=0, tiled=True)  79.2 us
    ppermute x17, starting transfers between devices, swap(): return lax.ppermute(value, 'tp', [(0, 1), (1, 0)])  24.2 us
    ppermute x4, waiting for transfers between devices, summed_everywhere(): lax.ppermute(value, 'fsdp', [(place, place ^ step) for place in range(fsd...  16.7 us
  transfers between devices with their start and end apart: 27, of which 25 were waited for; matrix products, arithmetic and copies ran while one was open for 7% of the time, Pallas kernels for 16%

profile of v2, /device:TPU:0, one launch (start us, length us, event | category | flops | bytes accessed | tf_op | source)
XLA Modules:
  0.0 536.6 jit_solution(11221812527873175437)
XLA Ops:
  18.2 9.8 %collective-permute-done = bf16[296,768]{1,0:T(8,128)(2,1)S(1)} collective-permute-done((bf16[296,768]{1,0:T(8,128)(2,1)S(1)}, bf16[296,768]{1,0:T(8,128)(2,1)S(1)}, u32[]{:S(2)}, u32[]{:S(2)}) %collective-permute-start) | collective-permute-done | bytes 454688 | tf_op jit(solution)/shard_map/ppermute | solution.py:38
  29.4 26.4 %all-gather.4.cloned.1.call-done.weight_ref.turned_ref = bf16[768,1536]{1,0:T(8,128)(2,1)} async-done(((bf16[48,1536]{1,0:T(8,128)(2,1)}), bf16[768,1536]{1,0:T(8,128)(2,1)}) %all-gather.4.cloned.1.call-update) | async-done | bytes 2359312 | tf_op jit(solution)/shard_map/all_gather | solution.py:52
  55.8 9.1 %attend.2 = (bf16[592,1152]{1,0:T(8,128)(2,1)}, bf16[592,384]{1,0:T(8,128)(2,1)}, bf16[296,768]{1,0:T(8,128)(2,1)}, f32[296,768]{1,0:T(8,128)}) custom-call(s32[1]{0:T(128)} %bitcast.place_ref, bf16[592,768]{1,0:T(8,128)(2,1)} %pad_maximum_fusion.1.hidden_ref, bf16[768,1536]{1,0:T(8,128)(2,1)} %all-gather.4.cloned.1.call-done.weight_ref.turned_ref, ...), custom_call_target="tpu_custom_call" | custom-call | bytes 3182592 | tf_op jit(solution)/shard_map/attend/pallas_call | solution.py:269
  66.4 11.3 %collective-permute-done.1 = bf16[296,768]{1,0:T(8,128)(2,1)S(1)} collective-permute-done((bf16[296,768]{1,0:T(8,128)(2,1)}, bf16[296,768]{1,0:T(8,128)(2,1)S(1)}, u32[]{:S(2)}, u32[]{:S(2)}) %collective-permute-start.1) | collective-permute-done | bytes 454688 | tf_op jit(solution)/shard_map/ppermute | solution.py:38
  81.8 9.7 %collective-permute-done.2.hidden_ref.hidden_other = bf16[296,768]{1,0:T(8,128)(2,1)S(1)} collective-permute-done((bf16[296,768]{1,0:T(8,128)(2,1)S(1)}, bf16[296,768]{1,0:T(8,128)(2,1)S(1)}, u32[]{:S(2)}, u32[]{:S(2)}) %collective-permute-start.2) | collective-permute-done | bytes 454688 | tf_op jit(solution)/shard_map/ppermute | solution.py:38
  91.5 18.4 %all-gather.6.cloned.1.call-done.up_ref.turned_ref = bf16[768,3072]{1,0:T(8,128)(2,1)} async-done(((bf16[48,3072]{1,0:T(8,128)(2,1)}), bf16[768,3072]{1,0:T(8,128)(2,1)}) %all-gather.6.cloned.1.call-update) | async-done | bytes 4718608 | tf_op jit(solution)/shard_map/all_gather | solution.py:52
  116.6 5.4 %mlp.4 = (bf16[296,1536]{1,0:T(8,128)(2,1)}, bf16[296,1536]{1,0:T(8,128)(2,1)}, f32[296,768]{1,0:T(8,128)}) custom-call(bf16[296,768]{1,0:T(8,128)(2,1)} %copy-done.5, bf16[768,3072]{1,0:T(8,128)(2,1)} %all-gather.6.cloned.1.call-done.up_ref.turned_ref, bf16[768,3072]{1,0:T(8,128)(2,1)} %all-gather.6.cloned.1.call-done.up_ref.turned_ref, ...), custom_call_target="tpu_custom_call" | custom-call | bytes 2727936 | tf_op jit(solution)/shard_map/mlp/pallas_call | solution.py:269
  121.9 5.9 %collective-permute-done.3 = bf16[296,768]{1,0:T(8,128)(2,1)S(1)} collective-permute-done((bf16[296,768]{1,0:T(8,128)(2,1)}, bf16[296,768]{1,0:T(8,128)(2,1)S(1)}, u32[]{:S(2)}, u32[]{:S(2)}) %collective-permute-start.3) | collective-permute-done | bytes 454688 | tf_op jit(solution)/shard_map/ppermute | solution.py:38
  132.0 9.8 %collective-permute-done.4 = bf16[296,768]{1,0:T(8,128)(2,1)S(1)} collective-permute-done((bf16[296,768]{1,0:T(8,128)(2,1)S(1)}, bf16[296,768]{1,0:T(8,128)(2,1)S(1)}, u32[]{:S(2)}, u32[]{:S(2)}) %collective-permute-start.4) | collective-permute-done | bytes 454688 | tf_op jit(solution)/shard_map/ppermute | solution.py:38
  143.1 34.3 %all-gather.8.cloned.1.call-done.weight_ref.turned_ref.up_ref = bf16[768,4608]{1,0:T(8,128)(2,1)} async-done(((bf16[48,4608]{1,0:T(8,128)(2,1)}), bf16[768,4608]{1,0:T(8,128)(2,1)}) %all-gather.8.cloned.1.call-update) | async-done | bytes 7077904 | tf_op jit(solution)/shard_map/all_gather | solution.py:52
  177.4 9.5 %attend.3 = (bf16[592,1152]{1,0:T(8,128)(2,1)}, bf16[592,384]{1,0:T(8,128)(2,1)}, bf16[296,768]{1,0:T(8,128)(2,1)}, f32[296,768]{1,0:T(8,128)}) custom-call(s32[1]{0:T(128)} %bitcast.place_ref, bf16[592,768]{1,0:T(8,128)(2,1)} %pad_maximum_fusion.2.hidden_ref, bf16[768,4608]{1,0:T(8,128)(2,1)} %all-gather.8.cloned.1.call-done.weight_ref.turned_ref.up_ref, ...), custom_call_target="tpu_custom_call" | custom-call | bytes 3182592 | tf_op jit(solution)/shard_map/attend/pallas_call | solution.py:269
  188.7 11.1 %collective-permute-done.5 = bf16[296,768]{1,0:T(8,128)(2,1)S(1)} collective-permute-done((bf16[296,768]{1,0:T(8,128)(2,1)}, bf16[296,768]{1,0:T(8,128)(2,1)S(1)}, u32[]{:S(2)}, u32[]{:S(2)}) %collective-permute-start.5) | collective-permute-done | bytes 454688 | tf_op jit(solution)/shard_map/ppermute | solution.py:38
  205.3 10.8 %collective-permute-done.6.hidden_ref.hidden_other = bf16[296,768]{1,0:T(8,128)(2,1)} collective-permute-done((bf16[296,768]{1,0:T(8,128)(2,1)S(1)}, bf16[296,768]{1,0:T(8,128)(2,1)}, u32[]{:S(2)}, u32[]{:S(2)}) %collective-permute-start.6) | collective-permute-done | bytes 454688 | tf_op jit(solution)/shard_map/ppermute | solution.py:38
  224.3 5.3 mlp_back.5
  236.9 5.5 %mlp_back.4 = (bf16[296,1536]{1,0:T(8,128)(2,1)}, f32[296,768]{1,0:T(8,128)}, f32[1,1536]{1,0:T(1,128)}) custom-call(bf16[296,768]{1,0:T(8,128)(2,1)} %copy-done.3, bf16[296,1536]{1,0:T(8,128)(2,1)} %get-tuple-element.59.slope_ref, bf16[768,4608]{1,0:T(8,128)(2,1)} %all-gather.8.cloned.1.call-done.weight_ref.turned_ref.up_ref, ...), custom_call_target="tpu_custom_call" | custom-call | bytes 1824768 | tf_op jit(solution)/shard_map/mlp_back/pallas_call | solution.py:269
  244.8 5.8 %collective-permute-done.7 = bf16[296,768]{1,0:T(8,128)(2,1)} collective-permute-done((bf16[296,768]{1,0:T(8,128)(2,1)}, bf16[296,768]{1,0:T(8,128)(2,1)}, u32[]{:S(2)}, u32[]{:S(2)}) %collective-permute-start.7) | collective-permute-done | bytes 454688 | tf_op jit(solution)/shard_map/ppermute | solution.py:38
  254.8 8.5 %collective-permute-done.10 = bf16[296,768]{1,0:T(8,128)(2,1)S(1)} collective-permute-done((bf16[296,768]{1,0:T(8,128)(2,1)S(1)}, bf16[296,768]{1,0:T(8,128)(2,1)S(1)}, u32[]{:S(2)}, u32[]{:S(2)}) %collective-permute-start.10) | collective-permute-done | bytes 454688 | tf_op jit(solution)/shard_map/ppermute | solution.py:38
  264.4 16.3 %attend_back.2 = (bf16[592,1152]{1,0:T(8,128)(2,1)}, bf16[296,768]{1,0:T(8,128)(2,1)}, f32[296,768]{1,0:T(8,128)}, f32[1,1152]{1,0:T(1,128)}) custom-call(s32[1]{0:T(128)} %bitcast.place_ref, bf16[592,768]{1,0:T(8,128)(2,1)} %pad_maximum_fusion.3.branch_ref, bf16[592,1152]{1,0:T(8,128)(2,1)} %get-tuple-element.63.qkv_ref, ...), custom_call_target="tpu_custom_call" | custom-call | bytes 2732544 | tf_op jit(solution)/shard_map/attend_back/pallas_call | solution.py:269
  280.6 5.6 %attend_grads.3 = bf16[768,1536]{1,0:T(8,128)(2,1)} custom-call(bf16[592,768]{1,0:T(8,128)(2,1)} %pad_maximum_fusion.2.hidden_ref, bf16[592,1152]{1,0:T(8,128)(2,1)} %get-tuple-element.79.stacked_ref, bf16[592,768]{1,0:T(8,128)(2,1)} %pad_maximum_fusion.3.branch_ref, bf16[592,384]{1,0:T(8,128)(2,1)} %get-tuple-element.80.mixed_ref), custom_call_target="tpu_custom_call" | custom-call | bytes 2359296 | tf_op jit(solution)/shard_map/attend_grads/pallas_call | solution.py:269
  286.4 9.8 %mlp_grads.3 = bf16[768,3072]{1,0:T(8,128)(2,1)} custom-call(bf16[296,768]{1,0:T(8,128)(2,1)} %copy-done.6, bf16[296,768]{1,0:T(8,128)(2,1)} %collective-permute-done.6.hidden_ref.hidden_other, bf16[296,1536]{1,0:T(8,128)(2,1)} %get-tuple-element.81.pre_own, bf16[296,1536]{1,0:T(8,128)(2,1)} %get-tuple-element.82.pre_other, bf16[296,768]{1,0:T(8,128)(2,1)} %copy-done.3, ...), custom_call_target="tpu_custom_call" | custom-call | bytes 4718592 | tf_op jit(solution)/shard_map/mlp_grads/pallas_call | solution.py:269
  297.9 7.9 %collective-permute-done.11 = bf16[296,768]{1,0:T(8,128)(2,1)S(1)} collective-permute-done((bf16[296,768]{1,0:T(8,128)(2,1)}, bf16[296,768]{1,0:T(8,128)(2,1)S(1)}, u32[]{:S(2)}, u32[]{:S(2)}) %collective-permute-start.11) | collective-permute-done | bytes 454688 | tf_op jit(solution)/shard_map/ppermute | solution.py:38
  309.0 7.0 %collective-permute-done.12.branch_ref.branch_other = bf16[296,768]{1,0:T(8,128)(2,1)S(1)} collective-permute-done((bf16[296,768]{1,0:T(8,128)(2,1)S(1)}, bf16[296,768]{1,0:T(8,128)(2,1)S(1)}, u32[]{:S(2)}, u32[]{:S(2)}) %collective-permute-start.12) | collective-permute-done | bytes 454688 | tf_op jit(solution)/shard_map/ppermute | solution.py:38
  323.5 5.6 %mlp_back.6 = (bf16[296,1536]{1,0:T(8,128)(2,1)}, f32[296,768]{1,0:T(8,128)}, f32[1,1536]{1,0:T(1,128)}) custom-call(bf16[296,768]{1,0:T(8,128)(2,1)} %copy-done.4, bf16[296,1536]{1,0:T(8,128)(2,1)} %get-tuple-element.66.slope_ref, bf16[768,3072]{1,0:T(8,128)(2,1)} %all-gather.6.cloned.1.call-done.up_ref.turned_ref, ...), custom_call_target="tpu_custom_call" | custom-call | bytes 1824768 | tf_op jit(solution)/shard_map/mlp_back/pallas_call | solution.py:269
  335.2 9.8 %mlp_grads.2 = bf16[768,3072]{1,0:T(8,128)(2,1)} custom-call(bf16[296,768]{1,0:T(8,128)(2,1)} %copy-done.5, bf16[296,768]{1,0:T(8,128)(2,1)} %copy-done.15, bf16[296,1536]{1,0:T(8,128)(2,1)} %get-tuple-element.73.pre_own, bf16[296,1536]{1,0:T(8,128)(2,1)} %get-tuple-element.74.pre_other, bf16[296,768]{1,0:T(8,128)(2,1)} %copy-done.4, ...), custom_call_target="tpu_custom_call" | custom-call | bytes 4718592 | tf_op jit(solution)/shard_map/mlp_grads/pallas_call | solution.py:269
  347.0 16.4 %attend_back.3 = (bf16[592,1152]{1,0:T(8,128)(2,1)}, bf16[296,768]{1,0:T(8,128)(2,1)}, f32[296,768]{1,0:T(8,128)}, f32[1,1152]{1,0:T(1,128)}) custom-call(s32[1]{0:T(128)} %bitcast.place_ref, bf16[592,768]{1,0:T(8,128)(2,1)} %pad_maximum_fusion.4.branch_ref, bf16[592,1152]{1,0:T(8,128)(2,1)} %get-tuple-element.70.qkv_ref, ...), custom_call_target="tpu_custom_call" | custom-call | bytes 2732544 | tf_op jit(solution)/shard_map/attend_back/pallas_call | solution.py:269
  363.4 5.8 %attend_grads.2 = bf16[768,1536]{1,0:T(8,128)(2,1)} custom-call(bf16[592,768]{1,0:T(8,128)(2,1)} %pad_maximum_fusion.1.hidden_ref, bf16[592,1152]{1,0:T(8,128)(2,1)} %get-tuple-element.77.stacked_ref, bf16[592,768]{1,0:T(8,128)(2,1)} %pad_maximum_fusion.4.branch_ref, bf16[592,384]{1,0:T(8,128)(2,1)} %get-tuple-element.78.mixed_ref), custom_call_target="tpu_custom_call" | custom-call | bytes 2359296 | tf_op jit(solution)/shard_map/attend_grads/pallas_call | solution.py:269
  369.3 6.7 %pad_maximum_fusion = bf16[768,4608]{1,0:T(8,128)(2,1)} fusion(bf16[768,1536]{1,0:T(8,128)(2,1)} %attend_grads.2, bf16[768,3072]{1,0:T(8,128)(2,1)} %mlp_grads.2), kind=kLoop, calls=%fused_computation | loop fusion | flops 14155776 | bytes 14155776 | tf_op jit(solution)/shard_map/concatenate | solution.py:496
  378.4 7.5 %collective-permute-done.15 = bf16[296,768]{1,0:T(8,128)(2,1)} collective-permute-done((bf16[296,768]{1,0:T(8,128)(2,1)}, bf16[296,768]{1,0:T(8,128)(2,1)}, u32[]{:S(2)}, u32[]{:S(2)}) %collective-permute-start.15) | collective-permute-done | bytes 454688 | tf_op jit(solution)/shard_map/ppermute | solution.py:38
  390.0 5.4 %collective-permute-done.17 = f32[24,768]{1,0:T(8,128)S(1)} collective-permute-done((f32[24,768]{1,0:T(8,128)S(1)}, f32[24,768]{1,0:T(8,128)S(1)}, u32[]{:S(2)}, u32[]{:S(2)}) %collective-permute-start.17) | collective-permute-done | bytes 73760 | tf_op jit(solution)/shard_map/ppermute | solution.py:44
  402.5 8.6 %collective-permute-done.19 = f32[24,768]{1,0:T(8,128)S(1)} collective-permute-done((f32[24,768]{1,0:T(8,128)S(1)}, f32[24,768]{1,0:T(8,128)S(1)}, u32[]{:S(2)}, u32[]{:S(2)}) %collective-permute-start.19) | collective-permute-done | bytes 73760 | tf_op jit(solution)/shard_map/ppermute | solution.py:44
  420.6 11.0 %reduce-scatter.8.cloned.1.call-done = bf16[48,3072]{1,0:T(8,128)(2,1)} async-done(((bf16[768,3072]{1,0:T(8,128)(2,1)}), bf16[48,3072]{1,0:T(8,128)(2,1)}) %reduce-scatter.8.cloned.1.call-update) | async-done | bytes 294928 | tf_op jit(solution)/shard_map/reduce_scatter | solution.py:56
  432.7 91.9 %reduce-scatter.4.cloned.1.call-done = bf16[48,4608]{1,0:T(8,128)(2,1)} async-done(((bf16[768,4608]{1,0:T(8,128)(2,1)}), bf16[48,4608]{1,0:T(8,128)(2,1)}) %reduce-scatter.4.cloned.1.call-update) | async-done | bytes 442384 | tf_op jit(solution)/shard_map/reduce_scatter | solution.py:56
  (230 shorter events, 109.4 us)
Async XLA Ops:
  7.2 48.6 %all-gather.4.cloned.1.call-start = ((), (), s32[]{:S(2)}) async-start(), calls=%async_computation.3 | async-start | bytes 2506752 | tf_op jit(solution)/shard_map/all_gather | solution.py:52
  9.9 100.1 %all-gather.6.cloned.1.call-start = ((), (), s32[]{:S(2)}) async-start(), calls=%async_computation.4 | async-start | bytes 5013504 | tf_op jit(solution)/shard_map/all_gather | solution.py:52
  12.7 164.7 %all-gather.8.cloned.1.call-start = ((), (), s32[]{:S(2)}) async-start(), calls=%async_computation.5 | async-start | bytes 7520256 | tf_op jit(solution)/shard_map/all_gather | solution.py:52
  13.7 405.0 %reduce-scatter.6.cloned.1.call-start = ((), (), s32[]{:S(2)}) async-start(), calls=%async_computation.7 | async-start | bytes 2506752 | tf_op jit(solution)/shard_map/reduce_scatter | solution.py:56
  14.6 13.5 %collective-permute-start = (bf16[296,768]{1,0:T(8,128)(2,1)S(1)}, bf16[296,768]{1,0:T(8,128)(2,1)S(1)}, u32[]{:S(2)}, u32[]{:S(2)}) collective-permute-start(bf16[296,768]{1,0:T(8,128)(2,1)S(1)} %fusion.7), channel_id=1, source_target_pairs={{0,1},{1,0},{2,3},{3,2},{4,5},{5,4},{6,7},{7,6},{8,9},{9,8},{10,11... | collective-permute-start | bytes 1363976 | tf_op jit(solution)/shard_map/ppermute | solution.py:38
  64.9 12.8 %collective-permute-start.1 = (bf16[296,768]{1,0:T(8,128)(2,1)}, bf16[296,768]{1,0:T(8,128)(2,1)S(1)}, u32[]{:S(2)}, u32[]{:S(2)}) collective-permute-start(bf16[296,768]{1,0:T(8,128)(2,1)} %get-tuple-element.52), channel_id=1, source_target_pairs={{0,1},{1,0},{2,3},{3,2},{4,5},{5,4},{6,7},{7,6},{8,9},{9,8},{10,11... | collective-permute-start | bytes 1363976 | tf_op jit(solution)/shard_map/ppermute | solution.py:38
  79.6 35.4 %copy-start.5 = (bf16[296,768]{1,0:T(8,128)(2,1)}, bf16[296,768]{1,0:T(8,128)(2,1)S(1)}, u32[]{:S(2)}) copy-start(bf16[296,768]{1,0:T(8,128)(2,1)S(1)} %add_convert_fusion.2.hidden_ref.hidden_own) | copy-start | bytes 1363972
  79.6 11.9 %collective-permute-start.2 = (bf16[296,768]{1,0:T(8,128)(2,1)S(1)}, bf16[296,768]{1,0:T(8,128)(2,1)S(1)}, u32[]{:S(2)}, u32[]{:S(2)}) collective-permute-start(bf16[296,768]{1,0:T(8,128)(2,1)S(1)} %add_convert_fusion.2.hidden_ref.hidden_own), channel_id=1, source_target_pairs={{0,1},{1,0},{2,3},{3,2},{4,5},{5,4},{6,7},{7,6},{8,9},{9,8},{10,11... | collective-permute-start | bytes 1363976 | tf_op jit(solution)/shard_map/ppermute | solution.py:38
  91.5 18.4 %copy-start.15 = (bf16[296,768]{1,0:T(8,128)(2,1)}, bf16[296,768]{1,0:T(8,128)(2,1)S(1)}, u32[]{:S(2)}) copy-start(bf16[296,768]{1,0:T(8,128)(2,1)S(1)} %collective-permute-done.2.hidden_ref.hidden_other) | copy-start | bytes 1363972
  115.1 12.8 %collective-permute-start.3 = (bf16[296,768]{1,0:T(8,128)(2,1)}, bf16[296,768]{1,0:T(8,128)(2,1)S(1)}, u32[]{:S(2)}, u32[]{:S(2)}) collective-permute-start(bf16[296,768]{1,0:T(8,128)(2,1)} %get-tuple-element.54), channel_id=1, source_target_pairs={{0,1},{1,0},{2,3},{3,2},{4,5},{5,4},{6,7},{7,6},{8,9},{9,8},{10,11... | collective-permute-start | bytes 1363976 | tf_op jit(solution)/shard_map/ppermute | solution.py:38
  129.8 11.9 %collective-permute-start.4 = (bf16[296,768]{1,0:T(8,128)(2,1)S(1)}, bf16[296,768]{1,0:T(8,128)(2,1)S(1)}, u32[]{:S(2)}, u32[]{:S(2)}) collective-permute-start(bf16[296,768]{1,0:T(8,128)(2,1)S(1)} %add_convert_fusion.1), channel_id=1, source_target_pairs={{0,1},{1,0},{2,3},{3,2},{4,5},{5,4},{6,7},{7,6},{8,9},{9,8},{10,11... | collective-permute-start | bytes 1363976 | tf_op jit(solution)/shard_map/ppermute | solution.py:38
  143.1 45.3 %copy-start.7 = (bf16[296,768]{1,0:T(8,128)(2,1)S(1)}, bf16[296,768]{1,0:T(8,128)(2,1)}, u32[]{:S(2)}) copy-start(bf16[296,768]{1,0:T(8,128)(2,1)} %param.21) | copy-start | bytes 1363972
  187.0 12.8 %collective-permute-start.5 = (bf16[296,768]{1,0:T(8,128)(2,1)}, bf16[296,768]{1,0:T(8,128)(2,1)S(1)}, u32[]{:S(2)}, u32[]{:S(2)}) collective-permute-start(bf16[296,768]{1,0:T(8,128)(2,1)} %get-tuple-element.56), channel_id=1, source_target_pairs={{0,1},{1,0},{2,3},{3,2},{4,5},{5,4},{6,7},{7,6},{8,9},{9,8},{10,11... | collective-permute-start | bytes 1363976 | tf_op jit(solution)/shard_map/ppermute | solution.py:38
  188.7 15.5 %copy-start.3 = (bf16[296,768]{1,0:T(8,128)(2,1)}, bf16[296,768]{1,0:T(8,128)(2,1)S(1)}, u32[]{:S(2)}) copy-start(bf16[296,768]{1,0:T(8,128)(2,1)S(1)} %get-tuple-element.127.branch_ref.branch_own) | copy-start | bytes 1363972
  202.6 13.5 %collective-permute-start.6 = (bf16[296,768]{1,0:T(8,128)(2,1)S(1)}, bf16[296,768]{1,0:T(8,128)(2,1)}, u32[]{:S(2)}, u32[]{:S(2)}) collective-permute-start(bf16[296,768]{1,0:T(8,128)(2,1)S(1)} %add_convert_fusion.hidden_ref.hidden_own), channel_id=1, source_target_pairs={{0,1},{1,0},{2,3},{3,2},{4,5},{5,4},{6,7},{7,6},{8,9},{9,8},{10,11... | collective-permute-start | bytes 1363976 | tf_op jit(solution)/shard_map/ppermute | solution.py:38
  204.2 20.1 %collective-permute-start.8 = (bf16[296,768]{1,0:T(8,128)(2,1)S(1)}, bf16[296,768]{1,0:T(8,128)(2,1)}, u32[]{:S(2)}, u32[]{:S(2)}) collective-permute-start(bf16[296,768]{1,0:T(8,128)(2,1)S(1)} %get-tuple-element.127.branch_ref.branch_own), channel_id=1, source_target_pairs={{0,1},{1,0},{2,3},{3,2},{4,5},{5,4},{6,7},{7,6},{8,9},{9,8},{10,11... | collective-permute-start | bytes 1363976 | tf_op jit(solution)/shard_map/ppermute | solution.py:38
  229.6 13.5 %collective-permute-start.9 = (bf16[296,768]{1,0:T(8,128)(2,1)}, bf16[296,768]{1,0:T(8,128)(2,1)S(1)}, u32[]{:S(2)}, u32[]{:S(2)}) collective-permute-start(bf16[296,768]{1,0:T(8,128)(2,1)} %get-tuple-element.62), channel_id=1, source_target_pairs={{0,1},{1,0},{2,3},{3,2},{4,5},{5,4},{6,7},{7,6},{8,9},{9,8},{10,11... | collective-permute-start | bytes 1363976 | tf_op jit(solution)/shard_map/ppermute | solution.py:38
  231.1 19.5 %collective-permute-start.7 = (bf16[296,768]{1,0:T(8,128)(2,1)}, bf16[296,768]{1,0:T(8,128)(2,1)}, u32[]{:S(2)}, u32[]{:S(2)}) collective-permute-start(bf16[296,768]{1,0:T(8,128)(2,1)} %get-tuple-element.58), channel_id=1, source_target_pairs={{0,1},{1,0},{2,3},{3,2},{4,5},{5,4},{6,7},{7,6},{8,9},{9,8},{10,11... | collective-permute-start | bytes 1363976 | tf_op jit(solution)/shard_map/ppermute | solution.py:38
  253.2 10.1 %collective-permute-start.10 = (bf16[296,768]{1,0:T(8,128)(2,1)S(1)}, bf16[296,768]{1,0:T(8,128)(2,1)S(1)}, u32[]{:S(2)}, u32[]{:S(2)}) collective-permute-start(bf16[296,768]{1,0:T(8,128)(2,1)S(1)} %get-tuple-element.129), channel_id=1, source_target_pairs={{0,1},{1,0},{2,3},{3,2},{4,5},{5,4},{6,7},{7,6},{8,9},{9,8},{10,11... | collective-permute-start | bytes 1363976 | tf_op jit(solution)/shard_map/ppermute | solution.py:38
  286.3 145.3 %reduce-scatter.8.cloned.1.call-start = ((), (), s32[]{:S(2)}) async-start(), calls=%async_computation.8 | async-start | bytes 5013504 | tf_op jit(solution)/shard_map/reduce_scatter | solution.py:56
  296.1 228.5 %reduce-scatter.4.cloned.1.call-start = ((), (), s32[]{:S(2)}) async-start(), calls=%async_computation.6 | async-start | bytes 7520256 | tf_op jit(solution)/shard_map/reduce_scatter | solution.py:56
  296.4 9.4 %collective-permute-start.11 = (bf16[296,768]{1,0:T(8,128)(2,1)}, bf16[296,768]{1,0:T(8,128)(2,1)S(1)}, u32[]{:S(2)}, u32[]{:S(2)}) collective-permute-start(bf16[296,768]{1,0:T(8,128)(2,1)} %get-tuple-element.65), channel_id=1, source_target_pairs={{0,1},{1,0},{2,3},{3,2},{4,5},{5,4},{6,7},{7,6},{8,9},{9,8},{10,11... | collective-permute-start | bytes 1363976 | tf_op jit(solution)/shard_map/ppermute | solution.py:38
  307.5 14.6 %copy-start.4 = (bf16[296,768]{1,0:T(8,128)(2,1)}, bf16[296,768]{1,0:T(8,128)(2,1)S(1)}, u32[]{:S(2)}) copy-start(bf16[296,768]{1,0:T(8,128)(2,1)S(1)} %get-tuple-element.131.branch_ref.branch_own) | copy-start | bytes 1363972
  307.5 8.5 %collective-permute-start.12 = (bf16[296,768]{1,0:T(8,128)(2,1)S(1)}, bf16[296,768]{1,0:T(8,128)(2,1)S(1)}, u32[]{:S(2)}, u32[]{:S(2)}) collective-permute-start(bf16[296,768]{1,0:T(8,128)(2,1)S(1)} %get-tuple-element.131.branch_ref.branch_own), channel_id=1, source_target_pairs={{0,1},{1,0},{2,3},{3,2},{4,5},{5,4},{6,7},{7,6},{8,9},{9,8},{10,11... | collective-permute-start | bytes 1363976 | tf_op jit(solution)/shard_map/ppermute | solution.py:38
  322.1 9.2 %collective-permute-start.13 = (bf16[296,768]{1,0:T(8,128)(2,1)}, bf16[296,768]{1,0:T(8,128)(2,1)S(1)}, u32[]{:S(2)}, u32[]{:S(2)}) collective-permute-start(bf16[296,768]{1,0:T(8,128)(2,1)} %get-tuple-element.69), channel_id=1, source_target_pairs={{0,1},{1,0},{2,3},{3,2},{4,5},{5,4},{6,7},{7,6},{8,9},{9,8},{10,11... | collective-permute-start | bytes 1363976 | tf_op jit(solution)/shard_map/ppermute | solution.py:38
  333.6 11.3 %collective-permute-start.14 = (bf16[296,768]{1,0:T(8,128)(2,1)S(1)}, bf16[296,768]{1,0:T(8,128)(2,1)}, u32[]{:S(2)}, u32[]{:S(2)}) collective-permute-start(bf16[296,768]{1,0:T(8,128)(2,1)S(1)} %get-tuple-element.134), channel_id=1, source_target_pairs={{0,1},{1,0},{2,3},{3,2},{4,5},{5,4},{6,7},{7,6},{8,9},{9,8},{10,11... | collective-permute-start | bytes 1363976 | tf_op jit(solution)/shard_map/ppermute | solution.py:38
  377.1 8.8 %collective-permute-start.15 = (bf16[296,768]{1,0:T(8,128)(2,1)}, bf16[296,768]{1,0:T(8,128)(2,1)}, u32[]{:S(2)}, u32[]{:S(2)}) collective-permute-start(bf16[296,768]{1,0:T(8,128)(2,1)} %get-tuple-element.72), channel_id=1, source_target_pairs={{0,1},{1,0},{2,3},{3,2},{4,5},{5,4},{6,7},{7,6},{8,9},{9,8},{10,11... | collective-permute-start | bytes 1363976 | tf_op jit(solution)/shard_map/ppermute | solution.py:38
  387.6 1.3 collective-permute-start.16
  388.9 6.6 %collective-permute-start.17 = (f32[24,768]{1,0:T(8,128)S(1)}, f32[24,768]{1,0:T(8,128)S(1)}, u32[]{:S(2)}, u32[]{:S(2)}) collective-permute-start(f32[24,768]{1,0:T(8,128)S(1)} %add.271), channel_id=1, source_target_pairs={{0,4},{2,6},{4,0},{6,2},{8,12},{10,14},{12,8},{14,10},{16,20},{18,... | collective-permute-start | bytes 221192 | tf_op jit(solution)/shard_map/ppermute | solution.py:44
  395.5 4.9 collective-permute-start.18
  400.4 10.7 %collective-permute-start.19 = (f32[24,768]{1,0:T(8,128)S(1)}, f32[24,768]{1,0:T(8,128)S(1)}, u32[]{:S(2)}, u32[]{:S(2)}) collective-permute-start(f32[24,768]{1,0:T(8,128)S(1)} %add.273), channel_id=1, source_target_pairs={{0,16},{2,18},{4,20},{6,22},{8,24},{10,26},{12,28},{14,30},{16,0},... | collective-permute-start | bytes 221192 | tf_op jit(solution)/shard_map/ppermute | solution.py:44
  411.1 4.4 collective-permute-start.20
  (25 other events, 106.1 us)
Sparse Core Ops, SparseCore 0:
  10.8 44.9 all-gather.3
  58.1 51.8 all-gather.5
  112.8 64.5 all-gather.7
  286.4 61.9 reduce-scatter.5
  352.2 79.4 reduce-scatter.7
  435.5 89.0 reduce-scatter.3
